TPU v7x, 32 devices: a whole 2x2x4 slice. The times are simulated.
32 devices in a mesh: batch: 8 (over z, x), mp: 4 (over y, core).
Axes of the slice: x: 2, y: 2, z: 4, core: 2. Of those that a mesh axis runs over, the one named last changes fastest.
Arguments:
- tokens: bfloat16 [16, 2048, 768], P('batch', 'mp'), may hold values from -6 to 6
- cotangent: bfloat16 [16, 2048, 768], P('batch', 'mp'), may hold values from -6 to 6
- lengths: int32 [16], P('batch'), may hold values from 64 to 2048, as said below
- pre_attn_gain: bfloat16 [768], replicated, may hold values from 0.099609375 to 1.8984375
- pre_attn_bias: bfloat16 [768], replicated, may hold values from -3 to 3
- qkv_weight: bfloat16 [3, 768, 768], replicated, may hold values from -0.21875 to 0.21875
- conv_weight: bfloat16 [3, 3, 768], replicated, may hold values from -3 to 3
- out_weight: bfloat16 [768, 768], replicated, may hold values from -1.5 to 1.5
- pre_ffn_gain: bfloat16 [768], replicated, may hold values from 0.099609375 to 1.8984375
- pre_ffn_bias: bfloat16 [768], replicated, may hold values from -3 to 3
- up_weight: bfloat16 [768, 3072], replicated, may hold values from -0.21875 to 0.21875
- up_bias: bfloat16 [3072], replicated, may hold values from -3 to 3
- down_weight: bfloat16 [3072, 768], replicated, may hold values from -0.109375 to 0.109375
- down_bias: bfloat16 [768], replicated, may hold values from -3 to 3
Outputs:
- output: bfloat16 [16, 2048, 768], P('batch', 'mp')
- tokens_grad: bfloat16 [16, 2048, 768], P('batch', 'mp')
- pre_attn_gain_grad: float32 [768], P(('batch', 'mp'))
- pre_attn_bias_grad: float32 [768], P(('batch', 'mp'))
- qkv_weight_grad: float32 [3, 768, 768], P(None, 'batch', 'mp')
- conv_weight_grad: float32 [3, 3, 768], P(None, None, ('batch', 'mp'))
- out_weight_grad: float32 [768, 768], P(('batch', 'mp'))
- pre_ffn_gain_grad: float32 [768], P(('batch', 'mp'))
- pre_ffn_bias_grad: float32 [768], P(('batch', 'mp'))
- up_weight_grad: float32 [768, 3072], P(('batch', 'mp'))
- up_bias_grad: float32 [3072], P(('batch', 'mp'))
- down_weight_grad: float32 [3072, 768], P(('batch', 'mp'))
- down_bias_grad: float32 [768], P(('batch', 'mp'))
Inputs may be any that keep to these rules, and one draw needn't show every extreme that they name: `lengths`: real tokens of each sequence; positions at or past it are padding. Some sequence has 2048 in every draw.
All inputs are finite; a program needn't handle non-finite values.
Results may differ from a plain program's by a relative error of at most 0.014.
The roundings to bfloat16 on the way count: a program that leaves them out, or rounds other values in their place, can miss the bound.
Values may be sent and summed in bfloat16 or wider, within the bound.
No kernel may reach another device: no remote copies, remote signals or barrier semaphores. Data moves between devices by JAX's collectives and lax.ppermute only.
A program may use at most 320 MiB of HBM per device.

v0:
```python
import jax
import jax.numpy as jnp
from jax import lax
from jax.sharding import PartitionSpec as P

HEAD_DIM = 64
QBLOCK = 512


EPSILON = 1e-05
NEGATIVE = -1000000000.0


def norm_forward(values, norm_gain, offset):
    center = values - jnp.mean(values, axis=-1, keepdims=True)
    inv_std = lax.rsqrt(jnp.mean(center * center, axis=-1, keepdims=True) + EPSILON)
    scaled = center * inv_std
    return (scaled * norm_gain + offset, scaled, inv_std)


def norm_backward(grad_out, norm_gain, scaled, inv_std):
    weighted = grad_out * norm_gain
    return inv_std * (
        weighted
        - jnp.mean(weighted, axis=-1, keepdims=True)
        - scaled * jnp.mean(weighted * scaled, axis=-1, keepdims=True)
    )


def conv_forward(values, kernel):
    taps = kernel.shape[1]
    seq_len = values.shape[0]
    padded = jnp.pad(values, ((taps - 1, 0), (0, 0), (0, 0)))
    total_sum = jnp.zeros(values.shape, jnp.float32)
    for offset in range(taps):
        first = taps - 1 - offset
        total_sum = total_sum + kernel[:, offset, :] * padded[first : first + seq_len]
    return (total_sum, padded)


def conv_backward(grad_mixed, kernel, padded):
    taps = kernel.shape[1]
    seq_len = grad_mixed.shape[0]
    grad_padded = jnp.pad(grad_mixed, ((0, taps - 1), (0, 0), (0, 0)))
    grad_values = jnp.zeros(grad_mixed.shape, jnp.float32)
    kernel_grads = []
    for offset in range(taps):
        first = taps - 1 - offset
        grad_values = grad_values + kernel[:, offset, :] * grad_padded[offset : offset + seq_len]
        kernel_grads.append(jnp.sum(grad_mixed * padded[first : first + seq_len], axis=0))
    return (grad_values, jnp.stack(kernel_grads, axis=1))


def block_scores(block_q, key_heads, first, length, key_pos):
    scores = jnp.einsum(
        "qhd,khd->hqk", block_q, key_heads, preferred_element_type=jnp.float32
    ) * HEAD_DIM ** (-0.5)
    query_pos = first + jnp.arange(block_q.shape[0], dtype=jnp.int32)
    allowed = (key_pos[None, :] <= query_pos[:, None]) & (key_pos[None, :] < length)
    return jnp.where(allowed[None], scores, NEGATIVE)


def attend_forward(mixed_b, length):
    seq_len = mixed_b.shape[0]
    head_vals = mixed_b.reshape(seq_len, 3, -1, HEAD_DIM)
    queries = head_vals[:, 0]
    key_heads = head_vals[:, 1]
    values = head_vals[:, 2]
    key_pos = jnp.arange(seq_len, dtype=jnp.int32)
    out_parts = []
    log_totals = []
    for first in range(0, seq_len, QBLOCK):
        scores = block_scores(queries[first : first + QBLOCK], key_heads, first, length, key_pos)
        log_total = jax.nn.logsumexp(scores, axis=-1, keepdims=True)
        prob_block = jnp.exp(scores - log_total).astype(jnp.bfloat16)
        out_parts.append(
            jnp.einsum("hqk,khd->qhd", prob_block, values, preferred_element_type=jnp.float32)
        )
        log_totals.append(log_total)
    return (jnp.concatenate(out_parts, axis=0).reshape(seq_len, -1), log_totals)


def attend_backward(mixed_b, grad_heads, log_totals, length):
    seq_len = mixed_b.shape[0]
    head_vals = mixed_b.reshape(seq_len, 3, -1, HEAD_DIM)
    queries = head_vals[:, 0]
    key_heads = head_vals[:, 1]
    values = head_vals[:, 2]
    grad_out = grad_heads.reshape(seq_len, -1, HEAD_DIM)
    key_pos = jnp.arange(seq_len, dtype=jnp.int32)
    scale = HEAD_DIM ** (-0.5)
    query_parts = []
    grad_keys = jnp.zeros(key_heads.shape, jnp.float32)
    grad_values = jnp.zeros(values.shape, jnp.float32)
    for block_index, first in enumerate(range(0, seq_len, QBLOCK)):
        block_q = queries[first : first + QBLOCK]
        scores = block_scores(block_q, key_heads, first, length, key_pos)
        prob_block = jnp.exp(scores - log_totals[block_index])
        block_grad = grad_out[first : first + QBLOCK]
        grad_values = grad_values + jnp.einsum(
            "hqk,qhd->khd",
            prob_block.astype(jnp.bfloat16),
            block_grad,
            preferred_element_type=jnp.float32,
        )
        grad_probs = jnp.einsum(
            "qhd,khd->hqk", block_grad, values, preferred_element_type=jnp.float32
        )
        row_delta = jnp.sum(grad_probs * prob_block, axis=-1, keepdims=True)
        grad_scores = (prob_block * (grad_probs - row_delta)).astype(jnp.bfloat16)
        query_parts.append(
            jnp.einsum("hqk,khd->qhd", grad_scores, key_heads, preferred_element_type=jnp.float32)
            * scale
        )
        grad_keys = (
            grad_keys
            + jnp.einsum("hqk,qhd->khd", grad_scores, block_q, preferred_element_type=jnp.float32)
            * scale
        )
    grad_queries = jnp.concatenate(query_parts, axis=0)
    return jnp.stack([grad_queries, grad_keys, grad_values], axis=1).reshape(seq_len, 3, -1)


def on_device(
    tokens,
    cotangent,
    lengths,
    pre_attn_gain,
    pre_attn_bias,
    qkv_weight,
    conv_weight,
    out_weight,
    pre_ffn_gain,
    pre_ffn_bias,
    up_weight,
    up_bias,
    down_weight,
    down_bias,
):
    groups = lax.axis_size("mp")
    member = lax.axis_index("mp")
    batch_groups = lax.axis_size("batch")
    local_rows = tokens.shape[1]
    model_width = tokens.shape[2]
    head_cols = model_width // groups
    col_start = member * head_cols
    taps = conv_weight.shape[1]
    kernel_own = lax.dynamic_slice_in_dim(conv_weight, col_start, head_cols, 2).astype(jnp.float32)
    gain_attn = pre_attn_gain.astype(jnp.float32)
    bias_attn = pre_attn_bias.astype(jnp.float32)
    gain_ffn = pre_ffn_gain.astype(jnp.float32)
    bias_ffn = pre_ffn_bias.astype(jnp.float32)
    up_bias_f = up_bias.astype(jnp.float32)
    down_bias_f = down_bias.astype(jnp.float32)
    row_pos = member * local_rows + jnp.arange(local_rows, dtype=jnp.int32)
    qkv_grad_shape = (3, model_width, model_width)

    def one_batch(running, inputs):
        seq_rows, grad_rows, length = inputs
        rows_f = seq_rows.astype(jnp.float32)
        valid_rows = (row_pos < length)[:, None]
        normed, scaled_attn, inv_attn = norm_forward(rows_f, gain_attn, bias_attn)
        normed_b = normed.astype(jnp.bfloat16)
        local_proj = jnp.einsum(
            "td,cde->tce", normed_b, qkv_weight, preferred_element_type=jnp.float32
        ).astype(jnp.bfloat16)
        projected_b = lax.all_to_all(local_proj, "mp", split_axis=2, concat_axis=0, tiled=True)
        mixed_f, padded = conv_forward(projected_b.astype(jnp.float32), kernel_own)
        mixed_b = mixed_f.astype(jnp.bfloat16)
        heads_out, log_totals = attend_forward(mixed_b, length)
        heads_tok = lax.all_to_all(
            heads_out.astype(jnp.bfloat16), "mp", split_axis=0, concat_axis=1, tiled=True
        )
        attended = jnp.dot(heads_tok, out_weight, preferred_element_type=jnp.float32)
        residual = rows_f + attended
        normed_ffn, scaled_ffn, inv_ffn = norm_forward(residual, gain_ffn, bias_ffn)
        normed_ffn_b = normed_ffn.astype(jnp.bfloat16)
        hidden_pre = (
            jnp.dot(normed_ffn_b, up_weight, preferred_element_type=jnp.float32) + up_bias_f
        )
        relu_part = jnp.maximum(hidden_pre, 0.0)
        activated = jnp.square(relu_part).astype(jnp.bfloat16)
        ffn_out = jnp.dot(activated, down_weight, preferred_element_type=jnp.float32) + down_bias_f
        result = jnp.where(valid_rows, residual + ffn_out, 0.0).astype(jnp.bfloat16)
        grad_y = jnp.where(valid_rows, grad_rows.astype(jnp.float32), 0.0)
        grad_ffn = grad_y.astype(jnp.bfloat16)
        grad_down = jnp.einsum("tf,td->fd", activated, grad_ffn, preferred_element_type=jnp.float32)
        grad_down_bias = jnp.sum(grad_ffn.astype(jnp.float32), axis=0)
        grad_act = jnp.einsum(
            "td,fd->tf", grad_ffn, down_weight, preferred_element_type=jnp.float32
        )
        grad_pre = (2.0 * relu_part * grad_act).astype(jnp.bfloat16)
        grad_up = jnp.einsum(
            "td,tf->df", normed_ffn_b, grad_pre, preferred_element_type=jnp.float32
        )
        grad_up_bias = jnp.sum(grad_pre.astype(jnp.float32), axis=0)
        grad_normed_ffn = jnp.einsum(
            "tf,df->td", grad_pre, up_weight, preferred_element_type=jnp.float32
        )
        grad_gain_ffn = jnp.sum(grad_normed_ffn * scaled_ffn, axis=0)
        grad_bias_ffn = jnp.sum(grad_normed_ffn, axis=0)
        grad_residual = grad_y + norm_backward(grad_normed_ffn, gain_ffn, scaled_ffn, inv_ffn)
        grad_attended = grad_residual.astype(jnp.bfloat16)
        grad_out_w = jnp.einsum(
            "te,td->ed", heads_tok, grad_attended, preferred_element_type=jnp.float32
        )
        grad_heads_tok = jnp.einsum(
            "td,ed->te", grad_attended, out_weight, preferred_element_type=jnp.float32
        ).astype(jnp.bfloat16)
        grad_heads = lax.all_to_all(grad_heads_tok, "mp", split_axis=1, concat_axis=0, tiled=True)
        grad_mixed = attend_backward(mixed_b, grad_heads, log_totals, length)
        grad_proj, grad_conv = conv_backward(grad_mixed, kernel_own, padded)
        grad_proj_b = grad_proj.astype(jnp.bfloat16)
        grad_proj_tok = lax.all_to_all(grad_proj_b, "mp", split_axis=0, concat_axis=2, tiled=True)
        grad_qkv = jnp.einsum(
            "td,tce->cde", normed_b, grad_proj_tok, preferred_element_type=jnp.float32
        )
        grad_normed = jnp.einsum(
            "tce,cde->td", grad_proj_tok, qkv_weight, preferred_element_type=jnp.float32
        )
        grad_gain_attn = jnp.sum(grad_normed * scaled_attn, axis=0)
        grad_bias_attn = jnp.sum(grad_normed, axis=0)
        grad_tokens = grad_residual + norm_backward(grad_normed, gain_attn, scaled_attn, inv_attn)
        updates = (
            grad_gain_attn,
            grad_bias_attn,
            grad_qkv,
            grad_conv,
            grad_out_w,
            grad_gain_ffn,
            grad_bias_ffn,
            grad_up,
            grad_up_bias,
            grad_down,
            grad_down_bias,
        )
        running = jax.tree.map(jnp.add, running, updates)
        return (running, (result, grad_tokens.astype(jnp.bfloat16)))

    start_grads = (
        jnp.zeros((model_width,), jnp.float32),
        jnp.zeros((model_width,), jnp.float32),
        jnp.zeros(qkv_grad_shape, jnp.float32),
        jnp.zeros((3, taps, head_cols), jnp.float32),
        jnp.zeros(out_weight.shape, jnp.float32),
        jnp.zeros((model_width,), jnp.float32),
        jnp.zeros((model_width,), jnp.float32),
        jnp.zeros(up_weight.shape, jnp.float32),
        jnp.zeros(up_bias.shape, jnp.float32),
        jnp.zeros(down_weight.shape, jnp.float32),
        jnp.zeros((model_width,), jnp.float32),
    )
    running, outputs = lax.scan(one_batch, start_grads, (tokens, cotangent, lengths))
    conv_full = lax.dynamic_update_slice_in_dim(
        jnp.zeros((3, taps, model_width), jnp.float32), running[3], col_start, 2
    )
    rows_part = model_width // batch_groups
    qkv_flat = (
        running[2]
        .reshape(3, batch_groups, rows_part, groups, head_cols)
        .transpose(1, 3, 0, 2, 4)
        .reshape(batch_groups * groups * 3 * rows_part, head_cols)
    )
    summed = (
        lax.psum_scatter(running[0], ("batch", "mp"), scatter_dimension=0, tiled=True),
        lax.psum_scatter(running[1], ("batch", "mp"), scatter_dimension=0, tiled=True),
        lax.psum_scatter(qkv_flat, ("batch", "mp"), scatter_dimension=0, tiled=True),
        lax.psum_scatter(conv_full, ("batch", "mp"), scatter_dimension=2, tiled=True),
        lax.psum_scatter(running[4], ("batch", "mp"), scatter_dimension=0, tiled=True),
        lax.psum_scatter(running[5], ("batch", "mp"), scatter_dimension=0, tiled=True),
        lax.psum_scatter(running[6], ("batch", "mp"), scatter_dimension=0, tiled=True),
        lax.psum_scatter(running[7], ("batch", "mp"), scatter_dimension=0, tiled=True),
        lax.psum_scatter(running[8], ("batch", "mp"), scatter_dimension=0, tiled=True),
        lax.psum_scatter(running[9], ("batch", "mp"), scatter_dimension=0, tiled=True),
        lax.psum_scatter(running[10], ("batch", "mp"), scatter_dimension=0, tiled=True),
    )
    qkv_sum = summed[2].reshape(3, rows_part, head_cols)
    return (
        outputs[0],
        outputs[1],
        summed[0],
        summed[1],
        qkv_sum,
        summed[3],
        summed[4],
        summed[5],
        summed[6],
        summed[7],
        summed[8],
        summed[9],
        summed[10],
    )


def solution(mesh):
    in_specs = (
        P("batch", "mp", None),
        P("batch", "mp", None),
        P("batch"),
        P(),
        P(),
        P(),
        P(),
        P(),
        P(),
        P(),
        P(),
        P(),
        P(),
        P(),
    )
    out_specs = (
        P("batch", "mp", None),
        P("batch", "mp", None),
        P(("batch", "mp")),
        P(("batch", "mp")),
        P(None, "batch", "mp"),
        P(None, None, ("batch", "mp")),
        P(("batch", "mp"), None),
        P(("batch", "mp")),
        P(("batch", "mp")),
        P(("batch", "mp"), None),
        P(("batch", "mp")),
        P(("batch", "mp"), None),
        P(("batch", "mp")),
    )
    return jax.shard_map(
        on_device, mesh=mesh, in_specs=in_specs, out_specs=out_specs, check_vma=False
    )
```

profile of v0, /device:TPU:0, one launch (start us, length us, event | category | flops | bytes accessed | tf_op | source)
XLA Modules:
  0.0 1405.1 jit_solution(3746548389037983586)
XLA Ops:
  13.4 859.4 %while.37 = (s32[]{:T(128)}, f32[768]{0:T(1024)}, f32[768]{0:T(1024)}, f32[3,768,768]{1,2,0:T(8,128)}, f32[3,3,192]{2,1,0:T(4,128)}, /*index=5*/f32[768,768]{1,0...) while((s32[]{:T(128)}, f32[768]{0:T(1024)}, ...), condition=%wide.region_30.31_spmd.clone, body=%wide.region_0.30_spmd.clone.sunk | while | flops 31852625920 | bytes 1296953600 | solution.py:253
  37.0 30.4 %all-to-all-done = bf16[512,3,768]{0,1,2:T(4,128)(2,1)} async-done(((bf16[512,3,768]{0,1,2:T(4,128)(2,1)}), bf16[512,3,768]{0,1,2:T(4,128)(2,1)}, u32[]{:S(2)}, u32[]{:S(2)}) %all-to-all-start) | async-done | bytes 2359328 | tf_op jit(solution)/shard_map/while/body/eval_jaxpr/all_to_all | solution.py:167
  161.4 10.9 all-to-all-done.1
  227.4 11.6 multiply_reduce_fusion.19
  287.0 10.3 multiply_reduce_fusion.22
  305.7 9.8 multiply_convert_fusion.19
  318.3 9.9 multiply_convert_fusion.18
  370.1 9.5 select_add_fusion.22
  392.6 25.7 %all-to-all-done.3 = bf16[2048,3,192]{2,1,0:T(4,128)(2,1)} async-done(((bf16[2048,3,192]{2,1,0:T(4,128)(2,1)}), bf16[2048,3,192]{2,1,0:T(4,128)(2,1)}, u32[]{:S(2)}, u32[]{:S(2)}) %all-to-all-start.3) | async-done | bytes 2359328 | tf_op jit(solution)/shard_map/while/body/eval_jaxpr/all_to_all | solution.py:214
  463.4 29.8 %all-to-all-done = bf16[512,3,768]{0,1,2:T(4,128)(2,1)} async-done(((bf16[512,3,768]{0,1,2:T(4,128)(2,1)}), bf16[512,3,768]{0,1,2:T(4,128)(2,1)}, u32[]{:S(2)}, u32[]{:S(2)}) %all-to-all-start) | async-done | bytes 2359328 | tf_op jit(solution)/shard_map/while/body/eval_jaxpr/all_to_all | solution.py:167
  587.2 10.9 all-to-all-done.1
  657.4 11.6 multiply_reduce_fusion.19
  716.9 10.3 multiply_reduce_fusion.22
  735.7 9.8 multiply_convert_fusion.19
  748.3 9.9 multiply_convert_fusion.18
  800.1 12.3 select_add_fusion.22
  825.3 22.9 %all-to-all-done.3 = bf16[2048,3,192]{2,1,0:T(4,128)(2,1)} async-done(((bf16[2048,3,192]{2,1,0:T(4,128)(2,1)}), bf16[2048,3,192]{2,1,0:T(4,128)(2,1)}, u32[]{:S(2)}, u32[]{:S(2)}) %all-to-all-start.3) | async-done | bytes 2359328 | tf_op jit(solution)/shard_map/while/body/eval_jaxpr/all_to_all | solution.py:214
  872.9 10.4 reshape.455
  883.3 10.2 copy.74
  895.2 41.7 %all-reduce.9 = (f32[768]{0:T(1024)S(1)}, f32[768]{0:T(1024)S(1)}, f32[3,3,768]{2,1,0:T(4,128)S(1)}, f32[768]{0:T(1024)S(1)}, f32[768]{0:T(1024)S(1)}, /*index=5*/f32[3072]{0:T(1024)S(1)}, f32[768]{0:T(1024)S(1)}) all-reduce(f32[768]{0:T(1024)S(1)} %copy-done.70, ...), channel_id=2, replica_groups=mesh['batch'=8,'mp'=4] {'batch','mp'}, use_global_device_ids=true, to_apply=%region_31.32.clone | all-reduce | flops 13824 | bytes 110592
  941.1 32.0 %reduce-scatter.8.cloned.1.call-done = f32[24,768]{1,0:T(8,128)} async-done(((f32[768,768]{1,0:T(8,128)}), f32[24,768]{1,0:T(8,128)}) %reduce-scatter.8.cloned.1.call-update) | async-done | bytes 73744 | tf_op jit(solution)/shard_map/reduce_scatter | solution.py:269
  973.1 142.0 %reduce-scatter.6.cloned.1.call-done = f32[288,192]{1,0:T(8,128)} async-done(((f32[9216,192]{1,0:T(8,128)}), f32[288,192]{1,0:T(8,128)}) %reduce-scatter.6.cloned.1.call-update) | async-done | bytes 221200 | tf_op jit(solution)/shard_map/reduce_scatter | solution.py:267
  1115.1 141.1 %reduce-scatter.10.cloned.1.call-done = f32[24,3072]{1,0:T(8,128)} async-done(((f32[768,3072]{1,0:T(8,128)}), f32[24,3072]{1,0:T(8,128)}) %reduce-scatter.10.cloned.1.call-update) | async-done | bytes 294928 | tf_op jit(solution)/shard_map/reduce_scatter | solution.py:272
  1256.3 142.0 %reduce-scatter.12.cloned.1.call-done = f32[96,768]{1,0:T(8,128)} async-done(((f32[3072,768]{1,0:T(8,128)}), f32[96,768]{1,0:T(8,128)}) %reduce-scatter.12.cloned.1.call-update) | async-done | bytes 294928 | tf_op jit(solution)/shard_map/reduce_scatter | solution.py:274
  (620 shorter events, 628.9 us)
Async XLA Ops:
  7.2 965.9 %reduce-scatter.8.cloned.1.call-start = ((), (), s32[]{:S(2)}) async-start(), calls=%async_computation.9 | async-start | bytes 2433024 | tf_op jit(solution)/shard_map/reduce_scatter | solution.py:269
  13.4 188.4 %copy-start.72 = (f32[768]{0:T(1024)}, f32[768]{0:T(1024)S(1)}, u32[]{:S(2)}) copy-start(f32[768]{0:T(1024)S(1)} %get-tuple-element.969) | copy-start | bytes 9220 | tf_op jit(solution)/shard_map/while
  13.4 196.3 %copy-start.37 = (f32[768]{0:T(1024)}, f32[768]{0:T(1024)S(1)}, u32[]{:S(2)}) copy-start(f32[768]{0:T(1024)S(1)} %get-tuple-element.964) | copy-start | bytes 9220 | tf_op jit(solution)/shard_map/while
  13.4 196.3 %copy-start.39 = (f32[768]{0:T(1024)}, f32[768]{0:T(1024)S(1)}, u32[]{:S(2)}) copy-start(f32[768]{0:T(1024)S(1)} %get-tuple-element.965) | copy-start | bytes 9220 | tf_op jit(solution)/shard_map/while
  24.9 42.4 %all-to-all-start = ((bf16[512,3,768]{0,1,2:T(4,128)(2,1)}), bf16[512,3,768]{0,1,2:T(4,128)(2,1)}, u32[]{:S(2)}, u32[]{:S(2)}) async-start(bf16[512,3,768]{0,1,2:T(4,128)(2,1)} %copy.93), calls=%async_computation | async-start | bytes 6291456 | tf_op jit(solution)/shard_map/while/body/eval_jaxpr/all_to_all | solution.py:167
  37.0 73.1 %copy-start.6 = (pred[512,2048]{1,0:T(8,128)(4,1)}, pred[512,2048]{1,0:T(8,128)(4,1)S(1)}, u32[]{:S(2)}) copy-start(pred[512,2048]{1,0:T(8,128)(4,1)S(1)} %get-tuple-element.837) | copy-start | bytes 3145732 | tf_op jit(solution)/shard_map/while
  37.0 92.6 %copy-start.9 = (pred[512,2048]{1,0:T(8,128)(4,1)}, pred[512,2048]{1,0:T(8,128)(4,1)S(1)}, u32[]{:S(2)}) copy-start(pred[512,2048]{1,0:T(8,128)(4,1)S(1)} %get-tuple-element.834) | copy-start | bytes 3145732 | tf_op jit(solution)/shard_map/while
  37.0 111.7 %copy-start.10 = (pred[512,2048]{1,0:T(8,128)(4,1)}, pred[512,2048]{1,0:T(8,128)(4,1)S(1)}, u32[]{:S(2)}) copy-start(pred[512,2048]{1,0:T(8,128)(4,1)S(1)} %get-tuple-element.831) | copy-start | bytes 3145732 | tf_op jit(solution)/shard_map/while
  156.8 15.5 %all-to-all-start.1 = ((bf16[4,512,192]{1,2,0:T(8,128)(2,1)}), bf16[4,512,192]{1,2,0:T(8,128)(2,1)S(1)}, u32[]{:S(2)}, u32[]{:S(2)}) async-start(bf16[4,512,192]{1,2,0:T(8,128)(2,1)} %copy.96), calls=%async_computation.1 | async-start | bytes 1572864 | tf_op jit(solution)/shard_map/while/body/eval_jaxpr/all_to_all | solution.py:171
  197.4 20.2 %all-to-all-start.2 = ((bf16[512,4,192]{0,2,1:T(8,128)(2,1)}), bf16[512,4,192]{0,2,1:T(8,128)(2,1)}, u32[]{:S(2)}, u32[]{:S(2)}) async-start(bf16[512,4,192]{0,2,1:T(8,128)(2,1)} %bitcast.484), calls=%async_computation.2 | async-start | bytes 1572864 | tf_op jit(solution)/shard_map/while/body/eval_jaxpr/all_to_all | solution.py:210
  364.8 53.4 %all-to-all-start.3 = ((bf16[2048,3,192]{2,1,0:T(4,128)(2,1)}), bf16[2048,3,192]{2,1,0:T(4,128)(2,1)}, u32[]{:S(2)}, u32[]{:S(2)}) async-start(bf16[2048,3,192]{2,1,0:T(4,128)(2,1)} %copy.98), calls=%async_computation.3 | async-start | bytes 8388608 | tf_op jit(solution)/shard_map/while/body/eval_jaxpr/all_to_all | solution.py:214
  439.8 187.8 %copy-start.72 = (f32[768]{0:T(1024)}, f32[768]{0:T(1024)S(1)}, u32[]{:S(2)}) copy-start(f32[768]{0:T(1024)S(1)} %get-tuple-element.969) | copy-start | bytes 9220 | tf_op jit(solution)/shard_map/while
  439.8 195.7 %copy-start.37 = (f32[768]{0:T(1024)}, f32[768]{0:T(1024)S(1)}, u32[]{:S(2)}) copy-start(f32[768]{0:T(1024)S(1)} %get-tuple-element.964) | copy-start | bytes 9220 | tf_op jit(solution)/shard_map/while
  439.8 195.7 %copy-start.39 = (f32[768]{0:T(1024)}, f32[768]{0:T(1024)S(1)}, u32[]{:S(2)}) copy-start(f32[768]{0:T(1024)S(1)} %get-tuple-element.965) | copy-start | bytes 9220 | tf_op jit(solution)/shard_map/while
  451.4 41.8 %all-to-all-start = ((bf16[512,3,768]{0,1,2:T(4,128)(2,1)}), bf16[512,3,768]{0,1,2:T(4,128)(2,1)}, u32[]{:S(2)}, u32[]{:S(2)}) async-start(bf16[512,3,768]{0,1,2:T(4,128)(2,1)} %copy.93), calls=%async_computation | async-start | bytes 6291456 | tf_op jit(solution)/shard_map/while/body/eval_jaxpr/all_to_all | solution.py:167
  463.4 91.9 %copy-start.9 = (pred[512,2048]{1,0:T(8,128)(4,1)}, pred[512,2048]{1,0:T(8,128)(4,1)S(1)}, u32[]{:S(2)}) copy-start(pred[512,2048]{1,0:T(8,128)(4,1)S(1)} %get-tuple-element.834) | copy-start | bytes 3145732 | tf_op jit(solution)/shard_map/while
  463.4 111.1 %copy-start.10 = (pred[512,2048]{1,0:T(8,128)(4,1)}, pred[512,2048]{1,0:T(8,128)(4,1)S(1)}, u32[]{:S(2)}) copy-start(pred[512,2048]{1,0:T(8,128)(4,1)S(1)} %get-tuple-element.831) | copy-start | bytes 3145732 | tf_op jit(solution)/shard_map/while
  582.7 15.5 %all-to-all-start.1 = ((bf16[4,512,192]{1,2,0:T(8,128)(2,1)}), bf16[4,512,192]{1,2,0:T(8,128)(2,1)S(1)}, u32[]{:S(2)}, u32[]{:S(2)}) async-start(bf16[4,512,192]{1,2,0:T(8,128)(2,1)} %copy.96), calls=%async_computation.1 | async-start | bytes 1572864 | tf_op jit(solution)/shard_map/while/body/eval_jaxpr/all_to_all | solution.py:171
  623.3 24.3 %all-to-all-start.2 = ((bf16[512,4,192]{0,2,1:T(8,128)(2,1)}), bf16[512,4,192]{0,2,1:T(8,128)(2,1)}, u32[]{:S(2)}, u32[]{:S(2)}) async-start(bf16[512,4,192]{0,2,1:T(8,128)(2,1)} %bitcast.484), calls=%async_computation.2 | async-start | bytes 1572864 | tf_op jit(solution)/shard_map/while/body/eval_jaxpr/all_to_all | solution.py:210
  794.8 53.4 %all-to-all-start.3 = ((bf16[2048,3,192]{2,1,0:T(4,128)(2,1)}), bf16[2048,3,192]{2,1,0:T(4,128)(2,1)}, u32[]{:S(2)}, u32[]{:S(2)}) async-start(bf16[2048,3,192]{2,1,0:T(4,128)(2,1)} %copy.98), calls=%async_computation.3 | async-start | bytes 8388608 | tf_op jit(solution)/shard_map/while/body/eval_jaxpr/all_to_all | solution.py:214
  872.8 242.3 %reduce-scatter.6.cloned.1.call-start = ((), (), s32[]{:S(2)}) async-start(), calls=%async_computation.8 | async-start | bytes 9732096 | tf_op jit(solution)/shard_map/reduce_scatter | solution.py:267
  893.5 362.8 %reduce-scatter.10.cloned.1.call-start = ((), (), s32[]{:S(2)}) async-start(), calls=%async_computation.10 | async-start | bytes 9732096 | tf_op jit(solution)/shard_map/reduce_scatter | solution.py:272
  894.2 504.0 %reduce-scatter.12.cloned.1.call-start = ((), (), s32[]{:S(2)}) async-start(), calls=%async_computation.11 | async-start | bytes 9732096 | tf_op jit(solution)/shard_map/reduce_scatter | solution.py:274
  894.3 504.0 %copy-start.1 = (bf16[3,3,768]{2,1,0:T(4,128)(2,1)S(1)}, bf16[3,3,768]{2,1,0:T(4,128)(2,1)}, u32[]{:S(2)}) copy-start(bf16[3,3,768]{2,1,0:T(4,128)(2,1)} %param.22) | copy-start | bytes 41476
  (170 other events, 1678.6 us)
Sparse Core Ops, SparseCore 0:
  872.9 100.1 reduce-scatter.7
  980.6 134.4 reduce-scatter.5
  1121.6 134.6 reduce-scatter.9
  1263.6 134.5 reduce-scatter.11
where the time goes:
time: 1410 us
  waiting for transfers between devices  589 us (42%)
  matrix products  409 us (29%)
  other arithmetic  180 us (13%)
  local copies, waits for them, and re-layouts  127 us (9%)
  blocking collectives  41.7 us (3%)
  starting transfers between devices  36.8 us (3%)
  between operations  14.4 us (1%)
    reduce_scatter x1, waiting for transfers between devices, on_device(): lax.psum_scatter(qkv_flat, ('batch', 'mp'), scatter_dimension=0, tiled=True)  142 us
    reduce_scatter x1, waiting for transfers between devices, on_device(): lax.psum_scatter(running[9], ('batch', 'mp'), scatter_dimension=0, tiled=...  142 us
    reduce_scatter x1, waiting for transfers between devices, on_device(): lax.psum_scatter(running[7], ('batch', 'mp'), scatter_dimension=0, tiled=...  141 us
    dot_general x8, matrix products, attend_backward(): jnp.einsum('qhd,khd->hqk', block_grad, values, preferred_element_type=jnp...  80.2 us
    convert_element_type x8, other arithmetic, attend_backward(): grad_scores = (prob_block * (grad_probs - row_delta)).astype(jnp.bfloat16)  71.2 us
    all_to_all x2, waiting for transfers between devices, one_batch(): lax.all_to_all(local_proj, 'mp', split_axis=2, concat_axis=0, tiled=True)  60.2 us
    dot_general x8, matrix products, attend_backward(): jnp.einsum('hqk,qhd->khd', prob_block.astype(jnp.bfloat16), block_grad, p...  59.4 us
    reduce_sum x8, other arithmetic, attend_forward(): log_total = jax.nn.logsumexp(scores, axis=-1, keepdims=True)  54.1 us
  transfers between devices with their start and end apart: 12, of which 10 were waited for; matrix products, arithmetic and copies ran while one was open for 9% of the time, Pallas kernels for 0%

commit v1 on v0

v1 whole, which is shorter than its diff:
```python
import functools

import jax
import jax.numpy as jnp
from jax import lax
from jax.experimental import pallas as pl
from jax.experimental.pallas import tpu as pltpu
from jax.sharding import PartitionSpec as P

HEAD_DIM = 64
LANES = 128
EPSILON = 1e-05
NEGATIVE = -1000000000.0
QBLOCK = 512
KBLOCK = 256
VMEM_BYTES = 60 << 20
F32 = jnp.float32
BF16 = jnp.bfloat16

CORE = [(i, i ^ 1) for i in range(4)]
PAIR = [(i, i ^ 2) for i in range(4)]


def dot_nt(left, right):
    return lax.dot_general(left, right, (((1,), (1,)), ((), ())), preferred_element_type=F32)


def dot_nn(left, right):
    return lax.dot_general(left, right, (((1,), (0,)), ((), ())), preferred_element_type=F32)


def dot_tn(left, right):
    return lax.dot_general(left, right, (((0,), (0,)), ((), ())), preferred_element_type=F32)


def params():
    return pltpu.CompilerParams(vmem_limit_bytes=VMEM_BYTES)


SMEM_SPEC = pl.BlockSpec(memory_space=pltpu.SMEM)


def norm_stats(values):
    center = values - jnp.mean(values, axis=-1, keepdims=True)
    inv_std = lax.rsqrt(jnp.mean(center * center, axis=-1, keepdims=True) + EPSILON)
    return center * inv_std, inv_std


def norm_backward(grad_out, norm_gain, scaled, inv_std):
    weighted = grad_out * norm_gain
    return inv_std * (
        weighted
        - jnp.mean(weighted, axis=-1, keepdims=True)
        - scaled * jnp.mean(weighted * scaled, axis=-1, keepdims=True)
    )


def project_kernel(x_ref, gain_ref, bias_ref, w_ref, normed_ref, proj_ref):
    scaled, _ = norm_stats(x_ref[...].astype(F32))
    normed = (scaled * gain_ref[...] + bias_ref[...]).astype(BF16)
    normed_ref[...] = normed
    proj_ref[...] = dot_nn(normed, w_ref[...]).astype(BF16)


def project(x, gain, bias, weight):
    rows, width = x.shape
    cols = weight.shape[1]
    tile = min(256, rows)
    return pl.pallas_call(
        project_kernel,
        grid=(rows // tile,),
        in_specs=[
            pl.BlockSpec((tile, width), lambda i: (i, 0)),
            pl.BlockSpec((1, width), lambda i: (0, 0)),
            pl.BlockSpec((1, width), lambda i: (0, 0)),
            pl.BlockSpec((width, cols), lambda i: (0, 0)),
        ],
        out_specs=[
            pl.BlockSpec((tile, width), lambda i: (i, 0)),
            pl.BlockSpec((tile, cols), lambda i: (i, 0)),
        ],
        out_shape=[
            jax.ShapeDtypeStruct((rows, width), BF16),
            jax.ShapeDtypeStruct((rows, cols), BF16),
        ],
        compiler_params=params(),
        cost_estimate=pl.CostEstimate(
            flops=2 * rows * width * cols, bytes_accessed=6 * rows * width, transcendentals=0
        ),
        name="project",
    )(x, gain, bias, weight)


def only_head(values, head):
    lane = lax.broadcasted_iota(jnp.int32, values.shape, 1)
    return jnp.where((lane // HEAD_DIM) == head, values, jnp.zeros_like(values))


def load_natural(member, blocks, dest, size, shift=0):
    for slot, block in enumerate(blocks):
        start = pl.multiple_of(lax.bitwise_xor(member, slot) * size, 8) + shift
        start = pl.multiple_of(start, 8)
        dest[pl.ds(start, size), :] = block.astype(dest.dtype)


def attend_kernel(
    m_ref, p0, p1, p2, p3, taps_ref, mixed_ref, own_ref, send_ref, lse_ref, pj, kh, vt, on, qs
):
    member = m_ref[0]
    size = p0.shape[0]
    length = 4 * size
    scale = jnp.asarray(HEAD_DIM ** (-0.5), BF16)
    for c in range(3):
        cols = slice(c * LANES, (c + 1) * LANES)
        pj[c, 0:8, :] = jnp.zeros((8, LANES), F32)
        load_natural(member, [p[:, cols] for p in (p0, p1, p2, p3)], pj.at[c], size, 8)
    for c in range(3):
        total = taps_ref[0, 3 * c : 3 * c + 1, :] * pj[c, 8 : 8 + length, :]
        total = total + taps_ref[0, 3 * c + 1 : 3 * c + 2, :] * pj[c, 7 : 7 + length, :]
        total = total + taps_ref[0, 3 * c + 2 : 3 * c + 3, :] * pj[c, 6 : 6 + length, :]
        mixed = total.astype(BF16)
        mixed_ref[:, c * LANES : (c + 1) * LANES] = mixed
        if c == 0:
            qs[...] = mixed * scale
        elif c == 1:
            kh[0] = only_head(mixed, 0)
            kh[1] = only_head(mixed, 1)
        else:
            vt[...] = mixed.T
    for first in range(0, length, QBLOCK):
        queries = qs[first : first + QBLOCK, :]
        keys = first + QBLOCK
        outs = []
        for head in range(2):
            scores = dot_nt(kh[head, 0:keys, :], queries)
            key_pos = lax.broadcasted_iota(jnp.int32, (QBLOCK, QBLOCK), 0)
            query_pos = lax.broadcasted_iota(jnp.int32, (QBLOCK, QBLOCK), 1)
            corner = jnp.where(key_pos <= query_pos, scores[first:keys, :], NEGATIVE)
            if first:
                scores = jnp.concatenate([scores[:first, :], corner], axis=0)
            else:
                scores = corner
            top = jnp.max(scores, axis=0, keepdims=True)
            weights = jnp.exp(scores - top)
            total = jnp.sum(weights, axis=0, keepdims=True)
            part = dot_nn(
                vt[head * HEAD_DIM : (head + 1) * HEAD_DIM, 0:keys], weights.astype(BF16)
            )
            outs.append(part * (1.0 / total))
            lse_ref[0, head : head + 1, first : first + QBLOCK] = top + jnp.log(total)
        on[first : first + QBLOCK, :] = jnp.concatenate(outs, axis=0).T.astype(BF16)
    for slot in range(4):
        start = pl.multiple_of(lax.bitwise_xor(member, slot) * size, size)
        block = on[pl.ds(start, size), :]
        dest = (own_ref, send_ref)[slot % 2]
        dest[slot // 2 * size : (slot // 2 + 1) * size, :] = block


def attend(member, proj, taps):
    size = proj[0].shape[0]
    pairs = proj[0].shape[1] // (3 * LANES)
    length = 4 * size
    width = pairs * LANES
    return pl.pallas_call(
        attend_kernel,
        grid=(pairs,),
        in_specs=[SMEM_SPEC]
        + [pl.BlockSpec((size, 3 * LANES), lambda p: (0, p))] * 4
        + [pl.BlockSpec((1, 16, LANES), lambda p: (p, 0, 0))],
        out_specs=[
            pl.BlockSpec((length, 3 * LANES), lambda p: (0, p)),
            pl.BlockSpec((2 * size, LANES), lambda p: (0, p)),
            pl.BlockSpec((2 * size, LANES), lambda p: (0, p)),
            pl.BlockSpec((1, 2, length), lambda p: (p, 0, 0)),
        ],
        out_shape=[
            jax.ShapeDtypeStruct((length, 3 * width), BF16),
            jax.ShapeDtypeStruct((2 * size, width), BF16),
            jax.ShapeDtypeStruct((2 * size, width), BF16),
            jax.ShapeDtypeStruct((pairs, 2, length), F32),
        ],
        scratch_shapes=[
            pltpu.VMEM((3, 8 + length, LANES), F32),
            pltpu.VMEM((2, length, LANES), BF16),
            pltpu.VMEM((LANES, length), BF16),
            pltpu.VMEM((length, LANES), BF16),
            pltpu.VMEM((length, LANES), BF16),
        ],
        compiler_params=params(),
        cost_estimate=pl.CostEstimate(
            flops=pairs * 14 * 10**9, bytes_accessed=12 << 20, transcendentals=0
        ),
        name="attend",
    )(member, *proj, taps)


def attend_back_kernel(
    m_ref,
    p0,
    p1,
    p2,
    p3,
    mixed_ref,
    lse_ref,
    taps_ref,
    own_ref,
    send_ref,
    down_ref,
    drecv_ref,
    gown_ref,
    gsend_ref,
    gconv_ref,
    pj,
    dm,
    qh,
    doh,
    kt,
    dl,
    dqa,
    nat,
):
    member = m_ref[0]
    size = p0.shape[0]
    length = 4 * size
    scale = jnp.asarray(HEAD_DIM ** (-0.5), BF16)
    halves = [slice(0, size), slice(size, 2 * size)]
    load_natural(
        member,
        [own_ref[halves[0]], send_ref[halves[0]], own_ref[halves[1]], send_ref[halves[1]]],
        nat.at[0],
        size,
    )
    load_natural(
        member,
        [down_ref[halves[0]], drecv_ref[halves[0]], down_ref[halves[1]], drecv_ref[halves[1]]],
        nat.at[1],
        size,
    )
    grads = nat[1]
    product = (grads.astype(F32) * nat[0].astype(F32)).T
    for head in range(2):
        dl[head : head + 1, :] = jnp.sum(
            product[head * HEAD_DIM : (head + 1) * HEAD_DIM, :], axis=0, keepdims=True
        )
        doh[head] = only_head(grads, head)
        qh[head] = only_head(mixed_ref[:, 0:LANES], head) * scale
    kt[...] = mixed_ref[:, LANES : 2 * LANES].T
    for c in range(3):
        cols = slice(c * LANES, (c + 1) * LANES)
        pj[c, 0:8, :] = jnp.zeros((8, LANES), F32)
        dm[c, length : length + 8, :] = jnp.zeros((8, LANES), F32)
        load_natural(member, [p[:, cols] for p in (p0, p1, p2, p3)], pj.at[c], size, 8)
    for first in range(0, length, KBLOCK):
        keys = mixed_ref[first : first + KBLOCK, LANES : 2 * LANES]
        values = mixed_ref[first : first + KBLOCK, 2 * LANES : 3 * LANES]
        sum_v = None
        sum_k = None
        for head in range(2):
            scores = dot_nt(keys, qh[head, first:, :])
            key_pos = lax.broadcasted_iota(jnp.int32, (KBLOCK, KBLOCK), 0)
            query_pos = lax.broadcasted_iota(jnp.int32, (KBLOCK, KBLOCK), 1)
            corner = jnp.where(key_pos <= query_pos, scores[:, :KBLOCK], NEGATIVE)
            if first + KBLOCK < length:
                scores = jnp.concatenate([corner, scores[:, KBLOCK:]], axis=1)
            else:
                scores = corner
            probs = jnp.exp(scores - lse_ref[0, head : head + 1, first:])
            grad_probs = dot_nt(values, doh[head, first:, :])
            grad_scores = (probs * (grad_probs - dl[head : head + 1, first:])).astype(BF16)
            part_v = dot_nn(probs.astype(BF16), doh[head, first:, :])
            part_k = dot_nn(grad_scores, qh[head, first:, :])
            sum_v = part_v if sum_v is None else sum_v + part_v
            sum_k = part_k if sum_k is None else sum_k + part_k
            lanes = slice(head * HEAD_DIM, (head + 1) * HEAD_DIM)
            part_q = dot_nn(kt[lanes, first : first + KBLOCK], grad_scores)
            if first == 0:
                dqa[lanes, :] = part_q
            else:
                dqa[lanes, first:] += part_q
        dm[1, first : first + KBLOCK, :] = sum_k
        dm[2, first : first + KBLOCK, :] = sum_v
    dm[0, 0:length, :] = dqa[...].T * HEAD_DIM ** (-0.5)
    for c in range(3):
        grad = dm[c, 0:length, :]
        for s in range(3):
            gconv_ref[3 * c + s : 3 * c + s + 1, :] = jnp.sum(
                grad * pj[c, 8 - s : 8 - s + length, :], axis=0, keepdims=True
            )
        total = taps_ref[0, 3 * c : 3 * c + 1, :] * grad
        total = total + taps_ref[0, 3 * c + 1 : 3 * c + 2, :] * dm[c, 1 : 1 + length, :]
        total = total + taps_ref[0, 3 * c + 2 : 3 * c + 3, :] * dm[c, 2 : 2 + length, :]
        nat[0] = total.astype(BF16)
        for slot in range(4):
            start = pl.multiple_of(lax.bitwise_xor(member, slot) * size, size)
            dest = (gown_ref, gsend_ref)[slot % 2]
            dest[slot // 2 * size : (slot // 2 + 1) * size, c * LANES : (c + 1) * LANES] = nat[
                0, pl.ds(start, size), :
            ]


def attend_back(pair, member, proj, mixed, lse, taps, own, send, grad_own, grad_recv):
    size = proj[0].shape[0]
    length = 4 * size
    half_spec = pl.BlockSpec((2 * size, LANES), lambda i: (0, pair))
    return pl.pallas_call(
        attend_back_kernel,
        grid=(1,),
        in_specs=[SMEM_SPEC]
        + [pl.BlockSpec((size, 3 * LANES), lambda i: (0, pair))] * 4
        + [
            pl.BlockSpec((length, 3 * LANES), lambda i: (0, pair)),
            pl.BlockSpec((1, 2, length), lambda i: (pair, 0, 0)),
            pl.BlockSpec((1, 16, LANES), lambda i: (pair, 0, 0)),
        ]
        + [half_spec] * 4,
        out_specs=[
            pl.BlockSpec((2 * size, 3 * LANES), lambda i: (0, 0)),
            pl.BlockSpec((2 * size, 3 * LANES), lambda i: (0, 0)),
            pl.BlockSpec((16, LANES), lambda i: (0, 0)),
        ],
        out_shape=[
            jax.ShapeDtypeStruct((2 * size, 3 * LANES), BF16),
            jax.ShapeDtypeStruct((2 * size, 3 * LANES), BF16),
            jax.ShapeDtypeStruct((16, LANES), F32),
        ],
        scratch_shapes=[
            pltpu.VMEM((3, 8 + length, LANES), F32),
            pltpu.VMEM((3, 8 + length, LANES), F32),
            pltpu.VMEM((2, length, LANES), BF16),
            pltpu.VMEM((2, length, LANES), BF16),
            pltpu.VMEM((LANES, length), BF16),
            pltpu.VMEM((8, length), F32),
            pltpu.VMEM((LANES, length), F32),
            pltpu.VMEM((2, length, LANES), BF16),
        ],
        compiler_params=params(),
        cost_estimate=pl.CostEstimate(
            flops=12 * 10**9, bytes_accessed=12 << 20, transcendentals=0
        ),
        name="attend_back",
    )(member, *proj, mixed, lse, taps, own, send, grad_own, grad_recv)


def ordered(chunks, order):
    bits = len(order)
    return [
        sum(((i >> (bits - 1 - n)) & 1) << order[n] for n in range(bits)) for i in range(chunks)
    ]


def split_store(m_ref, pieces, keep_ref, send_ref):
    flag = m_ref[0] == 0
    keep_ref[...] = jnp.where(flag, pieces[0], pieces[1]).astype(BF16).reshape(keep_ref.shape)
    send_ref[...] = jnp.where(flag, pieces[1], pieces[0]).astype(BF16).reshape(send_ref.shape)


def rows_kernel(order, m_ref, x_ref, y_ref, keep_ref, send_ref):
    total = dot_tn(x_ref[...], y_ref[...])
    chunks = 2 ** len(order)
    size = total.shape[0] // chunks
    pieces = []
    for k in ordered(chunks, order):
        for tile in range(total.shape[1] // LANES):
            pieces.append(
                total[k * size : (k + 1) * size, tile * LANES : (tile + 1) * LANES]
            )
    middle = len(pieces) // 2
    split_store(
        m_ref,
        [jnp.concatenate(pieces[:middle], axis=0), jnp.concatenate(pieces[middle:], axis=0)],
        keep_ref,
        send_ref,
    )


def rows_grad(flag, x, y, order, name):
    tokens, rows = x.shape
    cols = y.shape[1]
    chunks = 2 ** len(order)
    tile = 2 * LANES
    block = rows // chunks * 2
    out = jax.ShapeDtypeStruct((chunks // 2, rows * cols // chunks // LANES, LANES), BF16)
    spec = pl.BlockSpec((chunks // 2, block, LANES), lambda j: (0, j, 0))
    return pl.pallas_call(
        functools.partial(rows_kernel, order),
        grid=(cols // tile,),
        in_specs=[
            SMEM_SPEC,
            pl.BlockSpec((tokens, rows), lambda j: (0, 0)),
            pl.BlockSpec((tokens, tile), lambda j: (0, j)),
        ],
        out_specs=[spec, spec],
        out_shape=[out, out],
        compiler_params=params(),
        cost_estimate=pl.CostEstimate(
            flops=2 * tokens * rows * cols, bytes_accessed=16 << 20, transcendentals=0
        ),
        name=name,
    )(flag, x, y)


def rows_restore(flat, rows, cols):
    return flat.reshape(cols // (2 * LANES), 2, rows, LANES).transpose(2, 0, 1, 3).reshape(rows, cols)


def whole_kernel(order, m_ref, x_ref, y_ref, keep_ref, send_ref):
    total = dot_tn(x_ref[...], y_ref[...])
    chunks = 2 ** len(order)
    size = total.shape[0] // chunks
    pieces = [total[k * size : (k + 1) * size] for k in ordered(chunks, order)]
    middle = len(pieces) // 2
    split_store(
        m_ref,
        [jnp.concatenate(pieces[:middle], axis=0), jnp.concatenate(pieces[middle:], axis=0)],
        keep_ref,
        send_ref,
    )


def whole_grad(flag, x, y, order, tile, name):
    tokens, rows = x.shape
    cols = y.shape[1]
    chunks = 2 ** len(order)
    out = jax.ShapeDtypeStruct((chunks // 2, rows // chunks, cols), BF16)
    spec = pl.BlockSpec((chunks // 2, rows // chunks, tile), lambda j: (0, 0, j))
    return pl.pallas_call(
        functools.partial(whole_kernel, order),
        grid=(cols // tile,),
        in_specs=[
            SMEM_SPEC,
            pl.BlockSpec((tokens, rows), lambda j: (0, 0)),
            pl.BlockSpec((tokens, tile), lambda j: (0, j)),
        ],
        out_specs=[spec, spec],
        out_shape=[out, out],
        compiler_params=params(),
        cost_estimate=pl.CostEstimate(
            flops=2 * tokens * rows * cols, bytes_accessed=16 << 20, transcendentals=0
        ),
        name=name,
    )(flag, x, y)


def qkv_kernel(order, m_ref, n0, n1, n2, n3, gown_ref, gsend_ref, keep_ref, send_ref):
    size = n0.shape[0]
    total = dot_tn(n0[...], gown_ref[0:size, :])
    total = total + dot_tn(n2[...], gown_ref[size:, :])
    total = total + dot_tn(n1[...], gsend_ref[0:size, :])
    total = total + dot_tn(n3[...], gsend_ref[size:, :])
    chunks = 2 ** len(order)
    rows = total.shape[0] // chunks
    pieces = [total[k * rows : (k + 1) * rows] for k in ordered(chunks, order)]
    middle = chunks // 2
    split_store(
        m_ref,
        [jnp.concatenate(pieces[:middle], axis=0), jnp.concatenate(pieces[middle:], axis=0)],
        keep_ref,
        send_ref,
    )


def qkv_grad(flag, normed, grad_own, grad_send, order):
    rows = normed[0].shape[1]
    cols = grad_own.shape[1]
    chunks = 2 ** len(order)
    out = jax.ShapeDtypeStruct((chunks // 2, rows // chunks, cols), BF16)
    return pl.pallas_call(
        functools.partial(qkv_kernel, order),
        in_specs=[SMEM_SPEC] + [pl.BlockSpec(memory_space=pltpu.VMEM)] * 6,
        out_specs=[pl.BlockSpec(memory_space=pltpu.VMEM)] * 2,
        out_shape=[out, out],
        compiler_params=params(),
        cost_estimate=pl.CostEstimate(
            flops=8 * normed[0].shape[0] * rows * cols, bytes_accessed=8 << 20, transcendentals=0
        ),
        name="qkv_grad",
    )(flag, *normed, grad_own, grad_send)


def input_grad_kernel(
    o0, o1, o2, r0, r1, r2, wown_ref, woth_ref, x_ref, gres_ref, gain_ref, out_ref, sums_ref, buf
):
    for n, ref in enumerate((o0, o1, o2, r0, r1, r2)):
        buf[:, n * 3 * LANES : (n + 1) * 3 * LANES] = ref[...]
    cols = 9 * LANES
    grad = dot_nt(buf[:, :cols], wown_ref[...]) + dot_nt(buf[:, cols:], woth_ref[...])
    scaled, inv_std = norm_stats(x_ref[...].astype(F32))
    sums_ref[0:1, :] = jnp.sum(grad * scaled, axis=0, keepdims=True)
    sums_ref[1:2, :] = jnp.sum(grad, axis=0, keepdims=True)
    total = gres_ref[...] + norm_backward(grad, gain_ref[...], scaled, inv_std)
    out_ref[...] = total.astype(BF16)


def input_grad(slot, owns, recvs, w_own, w_oth, x, grad_residual, gain):
    rows, width = x.shape
    part = pl.BlockSpec((rows, 3 * LANES), lambda i: (slot, 0))
    full = lambda a: pl.BlockSpec(a.shape, lambda i: (0, 0))
    return pl.pallas_call(
        input_grad_kernel,
        grid=(1,),
        in_specs=[part] * 6
        + [full(w_own), full(w_oth), full(x)]
        + [pl.BlockSpec((rows, width), lambda i: (slot, 0)), full(gain)],
        out_specs=[
            pl.BlockSpec((rows, width), lambda i: (0, 0)),
            pl.BlockSpec((8, width), lambda i: (0, 0)),
        ],
        out_shape=[
            jax.ShapeDtypeStruct((rows, width), BF16),
            jax.ShapeDtypeStruct((8, width), F32),
        ],
        scratch_shapes=[pltpu.VMEM((rows, 18 * LANES), BF16)],
        compiler_params=params(),
        cost_estimate=pl.CostEstimate(
            flops=2 * rows * width * 18 * LANES, bytes_accessed=8 << 20, transcendentals=0
        ),
        name="input_grad",
    )(*owns, *recvs, w_own, w_oth, x, grad_residual, gain)


def halve(keep, recv, stages):
    parts = [(keep, 0), (recv, 0)]
    count = keep.shape[0]
    for axis, perm, bit in stages:
        count = count // 2

        def take(which):
            total = None
            for array, start in parts:
                piece = lax.dynamic_slice_in_dim(array, start + which * count, count, 0)
                piece = piece.astype(F32)
                total = piece if total is None else total + piece
            return total

        arrived = lax.ppermute(take(1 - bit).astype(BF16), axis, perm)
        parts = [(array, start + bit * count) for array, start in parts] + [(arrived, 0)]
    total = None
    for array, start in parts:
        piece = lax.dynamic_slice_in_dim(array, start, count, 0).astype(F32)
        total = piece if total is None else total + piece
    return total


def everyone(value, hops):
    for axis, perm in hops:
        value = value + lax.ppermute(value, axis, perm)
    return value


def on_device(
    tokens,
    cotangent,
    lengths,
    pre_attn_gain,
    pre_attn_bias,
    qkv_weight,
    conv_weight,
    out_weight,
    pre_ffn_gain,
    pre_ffn_bias,
    up_weight,
    up_bias,
    down_weight,
    down_bias,
):
    groups = lax.axis_size("mp")
    batch_groups = lax.axis_size("batch")
    devices = groups * batch_groups
    member = lax.axis_index("mp")
    batch = lax.axis_index("batch")
    seqs, rows, width = tokens.shape
    ff = up_weight.shape[1]
    quarter = width // groups
    assert groups == 4 and seqs == 2 and quarter % HEAD_DIM == 0
    fast = batch_groups == 8 and (width // devices) % 8 == 0
    half = member // 2
    core = member % 2
    me = member.astype(jnp.int32).reshape(1)
    gain_attn = pre_attn_gain.astype(F32).reshape(1, width)
    bias_attn = pre_attn_bias.astype(F32).reshape(1, width)
    gain_ffn = pre_ffn_gain.astype(F32)
    bias_ffn = pre_ffn_bias.astype(F32)

    def swap_core(value):
        return lax.ppermute(value, "mp", CORE)

    def swap_pair(value):
        return lax.ppermute(value, "mp", PAIR)

    def pick(value, index):
        return lax.dynamic_index_in_dim(value, index, 0, keepdims=False)

    tok_own = pick(tokens, half)
    tok_pair = swap_pair(pick(tokens, 1 - half))
    tok_core = swap_core(tok_own)
    tok_cross = swap_core(tok_pair)
    cot_pair = swap_pair(pick(cotangent, 1 - half))
    cot = jnp.concatenate([pick(cotangent, half), cot_pair], axis=0)
    length = pick(lengths, half)
    row = jnp.arange(rows, dtype=jnp.int32)
    row_pos = jnp.concatenate([member * rows + row, jnp.bitwise_xor(member, 2) * rows + row])
    valid = (row_pos < length)[:, None]

    pairs = width // 2 // LANES
    by_core = qkv_weight.reshape(3, width, 2, 2, quarter).transpose(3, 1, 0, 2, 4)
    by_core = by_core.reshape(2, width, 3, pairs, LANES).transpose(0, 1, 3, 2, 4)
    by_core = by_core.reshape(2, width, 3 * width // 2)
    w_own = pick(by_core, core)
    w_oth = pick(by_core, 1 - core)
    taps = conv_weight.shape[1]
    taps_own = pick(conv_weight.reshape(3, taps, 2, 2, quarter).transpose(3, 0, 1, 2, 4), core)
    taps_own = taps_own.astype(F32).reshape(3 * taps, pairs, LANES).transpose(1, 0, 2)
    taps_own = jnp.pad(taps_own, ((0, 0), (0, 16 - 3 * taps), (0, 0)))
    out_core = out_weight.reshape(2, 2, quarter, width).transpose(1, 0, 2, 3)
    out_core = out_core.reshape(2, width // 2, width)
    out_all = jnp.concatenate([pick(out_core, core), pick(out_core, 1 - core)], axis=0)

    toks = (tok_own, tok_core, tok_pair, tok_cross)
    normed, proj = zip(*[project(t, gain_attn, bias_attn, w_own) for t in toks])
    mixed, heads_own, heads_send, lse = attend(me, proj, taps_own)
    heads_recv = swap_core(heads_send)
    heads_all = jnp.concatenate([heads_own, heads_recv], axis=1)

    mine = jnp.concatenate([tok_own, tok_pair], axis=0).astype(F32)
    residual = mine + jnp.dot(heads_all, out_all, preferred_element_type=F32)
    scaled_ffn, inv_ffn = norm_stats(residual)
    normed_ffn = (scaled_ffn * gain_ffn + bias_ffn).astype(BF16)
    hidden_pre = jnp.dot(normed_ffn, up_weight, preferred_element_type=F32) + up_bias.astype(F32)
    relu_part = jnp.maximum(hidden_pre, 0.0)
    activated = jnp.square(relu_part).astype(BF16)
    ffn_out = jnp.dot(activated, down_weight, preferred_element_type=F32)
    ffn_out = ffn_out + down_bias.astype(F32)
    result = jnp.where(valid, residual + ffn_out, 0.0).astype(BF16)
    result_pair = swap_pair(result[rows:])
    grad_ffn = jnp.where(valid, cot, jnp.zeros_like(cot))
    grad_y = grad_ffn.astype(F32)
    grad_down_bias = jnp.sum(grad_y, axis=0)
    grad_act = jnp.einsum("td,fd->tf", grad_ffn, down_weight, preferred_element_type=F32)
    grad_pre = (2.0 * relu_part * grad_act).astype(BF16)
    grad_up_bias = jnp.sum(grad_pre.astype(F32), axis=0)
    grad_normed_ffn = jnp.einsum("tf,df->td", grad_pre, up_weight, preferred_element_type=F32)
    grad_gain_ffn = jnp.sum(grad_normed_ffn * scaled_ffn, axis=0)
    grad_bias_ffn = jnp.sum(grad_normed_ffn, axis=0)
    grad_residual = grad_y + norm_backward(grad_normed_ffn, gain_ffn, scaled_ffn, inv_ffn)
    grad_attended = grad_residual.astype(BF16)
    grad_heads = jnp.einsum("td,ed->te", grad_attended, out_all, preferred_element_type=F32)
    grad_heads = grad_heads.astype(BF16)
    grad_own = grad_heads[:, : width // 2]
    grad_recv = swap_core(grad_heads[:, width // 2 :])

    flat_core = core.astype(jnp.int32).reshape(1)
    g_own, g_send, g_recv, g_conv = [], [], [], []
    for pair in range(pairs):
        own, send, conv = attend_back(
            pair, me, proj, mixed, lse, taps_own, heads_own, heads_send, grad_own, grad_recv
        )
        g_own.append(own)
        g_send.append(send)
        g_recv.append(swap_core(send))
        g_conv.append(conv)
    grad_in_pair, sums_pair = input_grad(
        1, g_own, g_recv, w_own, w_oth, tok_pair, grad_residual, gain_attn
    )
    grad_in_back = swap_pair(grad_in_pair)
    grad_in_own, sums_own = input_grad(
        0, g_own, g_recv, w_own, w_oth, tok_own, grad_residual, gain_attn
    )

    def both(first, second):
        return jnp.stack([jnp.where(half == 0, first, second), jnp.where(half == 0, second, first)])

    result_all = both(result[:rows], result_pair)
    tokens_grad = both(grad_in_own, grad_in_back)

    sums = sums_pair + sums_own
    conv_own = jnp.stack(g_conv)[:, : 3 * taps].transpose(1, 0, 2).reshape(3, taps, 2, quarter)
    conv_full = jnp.zeros((3, taps, 2, 2, quarter), F32)
    conv_full = lax.dynamic_update_slice_in_dim(conv_full, conv_own[:, :, :, None], core, 3)
    conv_full = conv_full.reshape(3 * taps, width)
    early = jnp.concatenate(
        [
            grad_up_bias.reshape(ff // width, width),
            grad_down_bias[None],
            grad_gain_ffn[None],
            grad_bias_ffn[None],
        ],
        axis=0,
    )
    late = jnp.concatenate([sums[0:2], conv_full], axis=0)
    index = batch * groups + member
    share = width // devices

    if not fast:
        axes = ("batch", "mp")
        grad_up = jnp.einsum("td,tf->df", normed_ffn, grad_pre, preferred_element_type=F32)
        grad_down = jnp.einsum("tf,td->fd", activated, grad_ffn, preferred_element_type=F32)
        grad_out = jnp.einsum("te,td->ed", heads_all, grad_attended, preferred_element_type=F32)
        grad_out = grad_out.reshape(2, 2, quarter, width)
        grad_out = jnp.where(core == 0, grad_out, grad_out[::-1])
        grad_out = grad_out.transpose(1, 0, 2, 3).reshape(width, width)
        grad_qkv = 0.0
        for n, (norm, slot) in enumerate(zip(normed, (0, 0, 1, 1))):
            source = (g_own, g_send)[n % 2]
            grads = jnp.concatenate([g[slot * rows : (slot + 1) * rows] for g in source], axis=1)
            grad_qkv = grad_qkv + jnp.einsum("td,te->de", norm, grads, preferred_element_type=F32)
        grad_qkv = grad_qkv.reshape(width, pairs, 3, LANES).transpose(2, 0, 1, 3)
        grad_qkv = grad_qkv.reshape(3, width, 2, 1, quarter)
        qkv_full = jnp.zeros((3, width, 2, 2, quarter), F32)
        qkv_full = lax.dynamic_update_slice_in_dim(qkv_full, grad_qkv, core, 3)
        part = width // batch_groups
        qkv_flat = qkv_full.reshape(3, batch_groups, part, groups, quarter)
        qkv_flat = qkv_flat.transpose(1, 3, 0, 2, 4).reshape(devices * 3 * part, quarter)

        def scatter(value):
            return lax.psum_scatter(value, axes, scatter_dimension=0, tiled=True)

        early_sum = lax.psum(early, axes)
        late_sum = lax.psum(late, axes)
        qkv_out = scatter(qkv_flat).reshape(3, part, quarter)
        up_out, down_out, out_out = scatter(grad_up), scatter(grad_down), scatter(grad_out)
    else:
        bits = {
            "core": core,
            "pair": half,
            "x": batch % 2,
            "z0": batch // 2 % 2,
            "z1": batch // 4,
        }
        flip = {
            "core": ("mp", CORE),
            "pair": ("mp", PAIR),
            "x": ("batch", [(i, i ^ 1) for i in range(8)]),
            "z0": ("batch", [(i, i ^ 2) for i in range(8)]),
            "z1": ("batch", [(i, i ^ 4) for i in range(8)]),
        }
        place = {"core": 0, "pair": 1, "x": 2, "z0": 3, "z1": 4}
        hops = [flip[n] for n in ("core", "pair", "x", "z0", "z1")]

        def reduce(grads, names):
            keep, send = grads
            axis, perm = flip[names[0]]
            recv = lax.ppermute(send, axis, perm)
            return halve(keep, recv, [flip[n] + (bits[n],) for n in names[1:]])

        first = ("core", "pair", "x", "z0", "z1")
        second = ("core", "x", "pair", "z0", "z1")
        third = ("x", "z0", "z1")
        order_first = [place[n] for n in first]
        order_second = [place[n] for n in second]
        order_third = [place[n] - 2 for n in third]
        flag_core = flat_core
        flag_x = bits["x"].astype(jnp.int32).reshape(1)
        grads_down = whole_grad(
            flag_core, activated, grad_ffn, order_second, 2 * LANES, "down_grad"
        )
        grads_up = rows_grad(flag_core, normed_ffn, grad_pre, order_first, "up_grad")
        out_order = jnp.where(core == 0, 0, 1)
        heads_sorted = jnp.concatenate(
            [
                jnp.where(core == 0, heads_own, heads_recv)[:, :quarter],
                jnp.where(core == 0, heads_recv, heads_own)[:, :quarter],
                jnp.where(core == 0, heads_own, heads_recv)[:, quarter:],
                jnp.where(core == 0, heads_recv, heads_own)[:, quarter:],
            ],
            axis=1,
        )
        grads_out = rows_grad(flag_core, heads_sorted, grad_attended, order_second, "out_grad")
        down_out = reduce(grads_down, second).reshape(ff // devices, width)
        up_out = rows_restore(reduce(grads_up, first), share, ff)
        out_out = rows_restore(reduce(grads_out, second), share, width)
        qkv_parts = []
        for pair in range(pairs):
            grads = qkv_grad(flag_x, normed, g_own[pair], g_send[pair], order_third)
            total = reduce(grads, third)
            qkv_parts.append(total.reshape(width // batch_groups, 3, LANES))
        qkv_all = jnp.stack(qkv_parts, axis=1).transpose(2, 0, 1, 3)
        qkv_all = qkv_all.reshape(3, width // batch_groups, 2, quarter).transpose(2, 0, 1, 3)
        arrived = lax.ppermute(pick(qkv_all, 1 - half).astype(BF16), "mp", PAIR)
        qkv_out = pick(qkv_all, half) + arrived.astype(F32)
        early_sum = everyone(early, hops)
        late_sum = everyone(late, hops)

    def own_part(value):
        count = value.shape[0]
        return pick(value.reshape(count, devices, share).transpose(1, 0, 2), index)

    early_own = own_part(early_sum[ff // width :])
    late_own = own_part(late_sum)
    up_bias_own = pick(early_sum[: ff // width].reshape(devices, ff // devices), index)
    return (
        result_all,
        tokens_grad,
        late_own[0],
        late_own[1],
        qkv_out,
        late_own[2:].reshape(3, taps, share),
        out_out,
        early_own[1],
        early_own[2],
        up_out,
        up_bias_own,
        down_out,
        early_own[0],
    )


def solution(mesh):
    in_specs = (
        P("batch", "mp", None),
        P("batch", "mp", None),
        P("batch"),
    ) + (P(),) * 11
    out_specs = (
        P("batch", "mp", None),
        P("batch", "mp", None),
        P(("batch", "mp")),
        P(("batch", "mp")),
        P(None, "batch", "mp"),
        P(None, None, ("batch", "mp")),
        P(("batch", "mp"), None),
        P(("batch", "mp")),
        P(("batch", "mp")),
        P(("batch", "mp"), None),
        P(("batch", "mp")),
        P(("batch", "mp"), None),
        P(("batch", "mp")),
    )
    return jax.shard_map(
        on_device, mesh=mesh, in_specs=in_specs, out_specs=out_specs, check_vma=False
    )
```

time: 1410 us -> 415 us (0.29)
  waiting for transfers between devices: 589 us -> 87 us
  matrix products: 409 us -> 43.8 us
  Pallas kernels: 0 us -> 154 us
  other arithmetic: 180 us -> 50.8 us
  local copies, waits for them, and re-layouts: 127 us -> 29.2 us
  blocking collectives: 41.7 us -> 0 us
    reduce_scatter x4 -> x0, waiting for transfers between devices: 457 us -> none  [the longest x1 142 us: on_device(): lax.psum_scatter(qkv_flat, ('batch', 'mp'), scatter_dimension=0, tiled=True)]
    dot_general x72 -> x6, matrix products: 409 us -> 43.8 us  [the longest x1 10.2 us: on_device(): jnp.einsum('td,fd->tf', grad_ffn, down_weight, preferred_element_type=F32)]
    pallas_call x0 -> x16, Pallas kernels: none -> 154 us  [the longest x3 53.5 us: attend_back(): pl.pallas_call(attend_back_kernel, grid=(1,), in_specs=[SMEM_SPEC] + [pl....]
    all_to_all x8 -> x0, waiting for transfers between devices: 131 us -> none  [the longest x2 60.2 us: one_batch(): lax.all_to_all(local_proj, 'mp', split_axis=2, concat_axis=0, tiled=True)]
    ppermute x0 -> x46, waiting for transfers between devices: none -> 87 us  [the longest x18 35.9 us: halve(): arrived = lax.ppermute(take(1 - bit).astype(BF16), axis, perm)]
    reduce_sum x20 -> x2, other arithmetic: 69.9 us -> 2.32 us  [the longest x1 1.84 us: on_device(): grad_down_bias = jnp.sum(grad_y, axis=0)]
    convert_element_type x19 -> x24, other arithmetic: 92.9 us -> 29.3 us  [the longest x18 26.2 us: halve(): arrived = lax.ppermute(take(1 - bit).astype(BF16), axis, perm)]
    ppermute x0 -> x46, starting transfers between devices: none -> 41.8 us  [the longest x18 19.7 us: halve(): arrived = lax.ppermute(take(1 - bit).astype(BF16), axis, perm)]
  transfers between devices with their start and end apart: 12 -> 46, of which waited for: 10 -> 14; matrix products, arithmetic and copies ran while one was open for 9% -> 17% of each run, Pallas kernels for 0% -> 35%
where the time goes in v1:
time: 415 us; the launch traced here: 409 us
  Pallas kernels  154 us (37%)
  waiting for transfers between devices  87 us (21%)
  other arithmetic  50.8 us (12%)
  matrix products  43.8 us (11%)
  starting transfers between devices  41.8 us (10%)
  local copies, waits for them, and re-layouts  29.2 us (7%)
    pallas_call x3, Pallas kernels, attend_back(): pl.pallas_call(attend_back_kernel, grid=(1,), in_specs=[SMEM_SPEC] + [pl....  53.5 us
    ppermute x18, waiting for transfers between devices, halve(): arrived = lax.ppermute(take(1 - bit).astype(BF16), axis, perm)  35.9 us
    ppermute x10, waiting for transfers between devices, everyone(): value = value + lax.ppermute(value, axis, perm)  31 us
    pallas_call x1, Pallas kernels, attend(): pl.pallas_call(attend_kernel, grid=(pairs,), in_specs=[SMEM_SPEC] + [pl.B...  26.4 us
    convert_element_type x18, other arithmetic, halve(): arrived = lax.ppermute(take(1 - bit).astype(BF16), axis, perm)  26.2 us
    ppermute x18, starting transfers between devices, halve(): arrived = lax.ppermute(take(1 - bit).astype(BF16), axis, perm)  19.7 us
    pallas_call x2, Pallas kernels, rows_grad(): pl.pallas_call(functools.partial(rows_kernel, order), grid=(cols // tile,...  17.9 us
    ppermute x4, waiting for transfers between devices, swap_pair(): return lax.ppermute(value, 'mp', PAIR)  17.6 us
  transfers between devices with their start and end apart: 46, of which 14 were waited for; matrix products, arithmetic and copies ran while one was open for 17% of the time, Pallas kernels for 35%

profile of v1, /device:TPU:0, one launch (start us, length us, event | category | flops | bytes accessed | tf_op | source)
XLA Modules:
  0.0 408.8 jit_solution(10061711990105699031)
XLA Ops:
  6.2 17.6 %collective-permute-done.x_ref = bf16[512,768]{1,0:T(8,128)(2,1)} collective-permute-done((bf16[512,768]{1,0:T(8,128)(2,1)S(1)}, bf16[512,768]{1,0:T(8,128)(2,1)}, u32[]{:S(2)}, u32[]{:S(2)}) %collective-permute-start) | collective-permute-done | bytes 786464 | tf_op jit(solution)/shard_map/ppermute | solution.py:588
  39.1 4.3 %project.4 = (bf16[512,768]{1,0:T(8,128)(2,1)}, bf16[512,1152]{1,0:T(8,128)(2,1)}) custom-call(bf16[512,768]{1,0:T(8,128)(2,1)} %get-tuple-element.133.x_ref, f32[1,768]{1,0:T(1,128)} %reshape.187.gain_ref, f32[1,768]{1,0:T(1,128)} %reshape.189.bias_ref, bf16[768,1152]{1,0:T(8,128)(2,1)} %bitcast.85), custom_call_target="tpu_custom_call" | custom-call | flops 905969664 | bytes 2359296 | tf_op jit(solution)/shard_map/project/pallas_call | solution.py:69
  44.0 4.3 %project.6 = (bf16[512,768]{1,0:T(8,128)(2,1)}, bf16[512,1152]{1,0:T(8,128)(2,1)}) custom-call(bf16[512,768]{1,0:T(8,128)(2,1)} %collective-permute-done.x_ref, f32[1,768]{1,0:T(1,128)} %reshape.187.gain_ref, f32[1,768]{1,0:T(1,128)} %reshape.189.bias_ref, bf16[768,1152]{1,0:T(8,128)(2,1)} %bitcast.86), custom_call_target="tpu_custom_call" | custom-call | flops 905969664 | bytes 2359296 | tf_op jit(solution)/shard_map/project/pallas_call | solution.py:69
  48.3 4.3 %project.5 = (bf16[512,768]{1,0:T(8,128)(2,1)}, bf16[512,1152]{1,0:T(8,128)(2,1)}) custom-call(bf16[512,768]{1,0:T(8,128)(2,1)} %collective-permute-done.1.x_ref, f32[1,768]{1,0:T(1,128)} %reshape.187.gain_ref, f32[1,768]{1,0:T(1,128)} %reshape.189.bias_ref, bf16[768,1152]{1,0:T(8,128)(2,1)} %bitcast.87), custom_call_target="tpu_custom_call" | custom-call | flops 905969664 | bytes 2359296 | tf_op jit(solution)/shard_map/project/pallas_call | solution.py:69
  52.6 4.3 %project.7 = (bf16[512,768]{1,0:T(8,128)(2,1)}, bf16[512,1152]{1,0:T(8,128)(2,1)}) custom-call(bf16[512,768]{1,0:T(8,128)(2,1)} %collective-permute-done.2.x_ref, f32[1,768]{1,0:T(1,128)} %reshape.187.gain_ref, f32[1,768]{1,0:T(1,128)} %reshape.189.bias_ref, bf16[768,1152]{1,0:T(8,128)(2,1)} %bitcast.88), custom_call_target="tpu_custom_call" | custom-call | flops 905969664 | bytes 2359296 | tf_op jit(solution)/shard_map/project/pallas_call | solution.py:69
  56.9 26.4 %attend.1 = (bf16[2048,1152]{1,0:T(8,128)(2,1)}, bf16[1024,384]{1,0:T(8,128)(2,1)}, bf16[1024,384]{1,0:T(8,128)(2,1)}, f32[3,2,2048]{2,1,0:T(2,128)}) custom-call(s32[1]{0:T(128)} %bitcast.3.m_ref, bf16[512,1152]{1,0:T(8,128)(2,1)} %get-tuple-element.50.p0, bf16[512,1152]{1,0:T(8,128)(2,1)} %get-tuple-element.51.p1, bf16[512,1152]{1,0:T(8,128)(2,1)} %get-tuple-element.52.p2, ...), custom_call_target="tpu_custom_call" | custom-call | flops 41999998976 | bytes 12582912 | tf_op jit(solution)/shard_map/attend/pallas_call | solution.py:164
  95.8 9.7 %multiply_convert_fusion.1 = (bf16[1024,3072]{1,0:T(8,128)(2,1)}, f32[1024,3072]{1,0:T(8,128)}) fusion(f32[3072]{0:T(1024)S(1)} %convert_element_type.377, bf16[1024,768]{1,0:T(8,128)(2,1)S(1)} %add_convert_fusion.x_ref, bf16[768,3072]{1,0:T(8,128)(2,1)S(1)} %bitcast.109), kind=kOutput, calls=%fused_computation.2 | convolution fusion | flops 4844421120 | bytes 25178112 | tf_op jit(solution)/shard_map/dot_general | solution.py:628
  105.5 10.2 %convert_reduce_fusion = (f32[3072]{0:T(1024)S(1)}, bf16[1024,3072]{1,0:T(8,128)(2,1)}) fusion(bf16[1024,768]{1,0:T(8,128)(2,1)S(1)} %get-tuple-element.118.y_ref, bf16[3072,768]{1,0:T(8,128)(2,1)S(1)} %bitcast.107, f32[1024,3072]{1,0:T(8,128)} %get-tuple-element.149, f32[3072]{0:T(1024)S(1)} %convert_element_type.377), kind=kOutput, calls=%fused_computation | convolution fusion | flops 4853855232 | bytes 25190400 | tf_op jit(solution)/shard_map/td,fd->tf/dot_general | solution.py:638
  115.7 9.4 %select_convert_fusion = bf16[1024,768]{1,0:T(8,128)(2,1)} fusion(f32[1024,768]{1,0:T(8,128)S(1)} %get-tuple-element.147, bf16[1024,3072]{1,0:T(8,128)(2,1)} %get-tuple-element.148.x_ref, bf16[3072,768]{1,0:T(8,128)(2,1)} %param.26, f32[768]{0:T(1024)S(1)} %convert_element_type.379, pred[1024]{0:T(1024)(128)(4,1)S(1)} %add_compare_fusion), kind=kOutput, calls=%fused_computation.8 | convolution fusion | flops 4834983936 | bytes 15732736 | tf_op jit(solution)/shard_map/dot_general | solution.py:631
  125.1 10.3 %down_grad.1 = (bf16[16,96,768]{2,1,0:T(8,128)(2,1)}, bf16[16,96,768]{2,1,0:T(8,128)(2,1)}) custom-call(s32[1]{0:T(128)} %bitcast.35.m_ref, bf16[1024,3072]{1,0:T(8,128)(2,1)} %get-tuple-element.148.x_ref, bf16[1024,768]{1,0:T(8,128)(2,1)} %copy-done.1), custom_call_target="tpu_custom_call" | custom-call | flops 4831838208 | bytes 16777216 | tf_op jit(solution)/shard_map/down_grad/pallas_call | solution.py:426
  135.4 9.3 %multiply_reduce_fusion = (f32[768]{0:T(1024)S(1)}, f32[1024]{0:T(1024)S(1)}, f32[1024]{0:T(1024)S(1)}, f32[768]{0:T(1024)S(1)}, f32[1024,768]{1,0:T(8,128)S(1)}) fusion(f32[1024,768]{1,0:T(8,128)S(1)} %get-tuple-element.147, f32[1024]{0:T(1024)S(1)} %add_rsqrt_fusion, f32[1024]{0:T(1024)S(1)} %broadcast_multiply_fusion.2, ...), kind=kOutput, calls=%fused_computation.6 | convolution fusion | flops 4838912000 | bytes 17327104 | tf_op jit(solution)/shard_map/tf,df->td/dot_general | solution.py:641
  160.3 4.8 %out_grad.1 = (bf16[16,144,128]{2,1,0:T(8,128)(2,1)}, bf16[16,144,128]{2,1,0:T(8,128)(2,1)}) custom-call(s32[1]{0:T(128)} %bitcast.35.m_ref, bf16[1024,768]{1,0:T(8,128)(2,1)} %pad_maximum_fusion.2.x_ref, bf16[1024,768]{1,0:T(8,128)(2,1)} %copy-done.11), custom_call_target="tpu_custom_call" | custom-call | flops 1207959552 | bytes 16777216 | tf_op jit(solution)/shard_map/out_grad/pallas_call | solution.py:384
  168.3 13.1 %up_grad.1 = (bf16[16,576,128]{2,1,0:T(8,128)(2,1)}, bf16[16,576,128]{2,1,0:T(8,128)(2,1)}) custom-call(s32[1]{0:T(128)} %bitcast.35.m_ref, bf16[1024,768]{1,0:T(8,128)(2,1)} %copy-done.9, bf16[1024,3072]{1,0:T(8,128)(2,1)} %get-tuple-element.152.y_ref), custom_call_target="tpu_custom_call" | custom-call | flops 4831838208 | bytes 16777216 | tf_op jit(solution)/shard_map/up_grad/pallas_call | solution.py:384
  186.5 17.8 %attend_back.5 = (bf16[1024,384]{1,0:T(8,128)(2,1)}, bf16[1024,384]{1,0:T(8,128)(2,1)}, f32[16,128]{1,0:T(8,128)}) custom-call(s32[1]{0:T(128)} %bitcast.3.m_ref, bf16[512,1152]{1,0:T(8,128)(2,1)} %get-tuple-element.50.p0, bf16[512,1152]{1,0:T(8,128)(2,1)} %get-tuple-element.51.p1, bf16[512,1152]{1,0:T(8,128)(2,1)} %get-tuple-element.52.p2, ...), custom_call_target="tpu_custom_call" | custom-call | flops 12000000000 | bytes 12582912 | tf_op jit(solution)/shard_map/attend_back/pallas_call | solution.py:305
  204.3 4.9 %qkv_grad.5 = (bf16[4,96,384]{2,1,0:T(8,128)(2,1)}, bf16[4,96,384]{2,1,0:T(8,128)(2,1)}) custom-call(s32[1]{0:T(128)} %bitcast.30.m_ref, bf16[512,768]{1,0:T(8,128)(2,1)} %get-tuple-element.71.n0, bf16[512,768]{1,0:T(8,128)(2,1)} %get-tuple-element.72.n1, bf16[512,768]{1,0:T(8,128)(2,1)} %get-tuple-element.73.n2, bf16[512,768]{1,0:T(8,128)(2,1)} %get-tuple-element.74.n3, ...), custom_call_target="tpu_custom_call" | custom-call | flops 1207959552 | bytes 8388608 | tf_op jit(solution)/shard_map/qkv_grad/pallas_call | solution.py:467
  209.8 18.0 %attend_back.4 = (bf16[1024,384]{1,0:T(8,128)(2,1)}, bf16[1024,384]{1,0:T(8,128)(2,1)}, f32[16,128]{1,0:T(8,128)}) custom-call(s32[1]{0:T(128)} %bitcast.3.m_ref, bf16[512,1152]{1,0:T(8,128)(2,1)} %get-tuple-element.50.p0, bf16[512,1152]{1,0:T(8,128)(2,1)} %get-tuple-element.51.p1, bf16[512,1152]{1,0:T(8,128)(2,1)} %get-tuple-element.52.p2, ...), custom_call_target="tpu_custom_call" | custom-call | flops 12000000000 | bytes 12582912 | tf_op jit(solution)/shard_map/attend_back/pallas_call | solution.py:305
  227.8 17.7 %attend_back.3 = (bf16[1024,384]{1,0:T(8,128)(2,1)}, bf16[1024,384]{1,0:T(8,128)(2,1)}, f32[16,128]{1,0:T(8,128)}) custom-call(s32[1]{0:T(128)} %bitcast.3.m_ref, bf16[512,1152]{1,0:T(8,128)(2,1)} %get-tuple-element.50.p0, bf16[512,1152]{1,0:T(8,128)(2,1)} %get-tuple-element.51.p1, bf16[512,1152]{1,0:T(8,128)(2,1)} %get-tuple-element.52.p2, ...), custom_call_target="tpu_custom_call" | custom-call | flops 12000000000 | bytes 12582912 | tf_op jit(solution)/shard_map/attend_back/pallas_call | solution.py:305
  245.5 4.9 %qkv_grad.4 = (bf16[4,96,384]{2,1,0:T(8,128)(2,1)}, bf16[4,96,384]{2,1,0:T(8,128)(2,1)}) custom-call(s32[1]{0:T(128)} %bitcast.30.m_ref, bf16[512,768]{1,0:T(8,128)(2,1)} %get-tuple-element.71.n0, bf16[512,768]{1,0:T(8,128)(2,1)} %get-tuple-element.72.n1, bf16[512,768]{1,0:T(8,128)(2,1)} %get-tuple-element.73.n2, bf16[512,768]{1,0:T(8,128)(2,1)} %get-tuple-element.74.n3, ...), custom_call_target="tpu_custom_call" | custom-call | flops 1207959552 | bytes 8388608 | tf_op jit(solution)/shard_map/qkv_grad/pallas_call | solution.py:467
  256.5 5.0 %qkv_grad.3 = (bf16[4,96,384]{2,1,0:T(8,128)(2,1)}, bf16[4,96,384]{2,1,0:T(8,128)(2,1)}) custom-call(s32[1]{0:T(128)} %bitcast.30.m_ref, bf16[512,768]{1,0:T(8,128)(2,1)} %get-tuple-element.71.n0, bf16[512,768]{1,0:T(8,128)(2,1)} %get-tuple-element.72.n1, bf16[512,768]{1,0:T(8,128)(2,1)} %get-tuple-element.73.n2, bf16[512,768]{1,0:T(8,128)(2,1)} %get-tuple-element.74.n3, ...), custom_call_target="tpu_custom_call" | custom-call | flops 1207959552 | bytes 8388608 | tf_op jit(solution)/shard_map/qkv_grad/pallas_call | solution.py:467
  294.2 7.0 %input_grad.3 = (bf16[512,768]{1,0:T(8,128)(2,1)}, f32[8,768]{1,0:T(8,128)}) custom-call(bf16[1024,384]{1,0:T(8,128)(2,1)} %get-tuple-element.58.o0.gown_ref, bf16[1024,384]{1,0:T(8,128)(2,1)} %get-tuple-element.59.o1.gown_ref, bf16[1024,384]{1,0:T(8,128)(2,1)} %get-tuple-element.60.o2.gown_ref, bf16[1024,384]{1,0:T(8,128)(2,1)} %collective-permute-done.7.r0, ...), custom_call_target="tpu_custom_call" | custom-call | flops 1811939328 | bytes 8388608 | tf_op jit(solution)/shard_map/input_grad/pallas_call | solution.py:498
  301.2 7.1 %input_grad.2 = (bf16[512,768]{1,0:T(8,128)(2,1)}, f32[8,768]{1,0:T(8,128)}) custom-call(bf16[1024,384]{1,0:T(8,128)(2,1)} %get-tuple-element.58.o0.gown_ref, bf16[1024,384]{1,0:T(8,128)(2,1)} %get-tuple-element.59.o1.gown_ref, bf16[1024,384]{1,0:T(8,128)(2,1)} %get-tuple-element.60.o2.gown_ref, bf16[1024,384]{1,0:T(8,128)(2,1)} %collective-permute-done.7.r0, ...), custom_call_target="tpu_custom_call" | custom-call | flops 1811939328 | bytes 8388608 | tf_op jit(solution)/shard_map/input_grad/pallas_call | solution.py:498
  319.7 22.8 %collective-permute-done.12 = f32[11,768]{1,0:T(8,128)S(1)} collective-permute-done((f32[11,768]{1,0:T(8,128)S(1)}, f32[11,768]{1,0:T(8,128)S(1)}, u32[]{:S(2)}, u32[]{:S(2)}) %collective-permute-start.12) | collective-permute-done | bytes 33824 | tf_op jit(solution)/shard_map/ppermute | solution.py:546
  362.6 18.3 %collective-permute-done.43 = bf16[4,96,768]{2,1,0:T(8,128)(2,1)} collective-permute-done((bf16[4,96,768]{2,1,0:T(8,128)(2,1)}, bf16[4,96,768]{2,1,0:T(8,128)(2,1)}, u32[]{:S(2)}, u32[]{:S(2)}) %collective-permute-start.43) | collective-permute-done | bytes 589856 | tf_op jit(solution)/shard_map/ppermute | solution.py:535
  387.2 6.4 %collective-permute-done.39 = bf16[2,576,128]{2,1,0:T(8,128)(2,1)S(1)} collective-permute-done((bf16[2,576,128]{2,1,0:T(8,128)(2,1)S(1)}, bf16[2,576,128]{2,1,0:T(8,128)(2,1)S(1)}, u32[]{:S(2)}, u32[]{:S(2)}) %collective-permute-start.39) | collective-permute-done | bytes 294944 | tf_op jit(solution)/shard_map/ppermute | solution.py:535
  (290 shorter events, 148.8 us)
Async XLA Ops:
  3.2 20.6 %collective-permute-start = (bf16[512,768]{1,0:T(8,128)(2,1)S(1)}, bf16[512,768]{1,0:T(8,128)(2,1)}, u32[]{:S(2)}, u32[]{:S(2)}) collective-permute-start(bf16[512,768]{1,0:T(8,128)(2,1)S(1)} %get-tuple-element.134), channel_id=1, source_target_pairs={{0,2},{1,3},{2,0},{3,1},{4,6},{5,7},{6,4},{7,5},{8,10},{9,11},{10,... | collective-permute-start | bytes 2359304 | tf_op jit(solution)/shard_map/ppermute | solution.py:588
  6.2 42.1 %collective-permute-start.1 = (bf16[512,768]{1,0:T(8,128)(2,1)}, bf16[512,768]{1,0:T(8,128)(2,1)}, u32[]{:S(2)}, u32[]{:S(2)}) collective-permute-start(bf16[512,768]{1,0:T(8,128)(2,1)} %get-tuple-element.133.x_ref), channel_id=1, source_target_pairs={{0,1},{1,0},{2,3},{3,2},{4,5},{5,4},{6,7},{7,6},{8,9},{9,8},{10,11... | collective-permute-start | bytes 2359304 | tf_op jit(solution)/shard_map/ppermute | solution.py:585
  23.8 28.8 %collective-permute-start.2 = (bf16[512,768]{1,0:T(8,128)(2,1)}, bf16[512,768]{1,0:T(8,128)(2,1)}, u32[]{:S(2)}, u32[]{:S(2)}) collective-permute-start(bf16[512,768]{1,0:T(8,128)(2,1)} %collective-permute-done.x_ref), channel_id=1, source_target_pairs={{0,1},{1,0},{2,3},{3,2},{4,5},{5,4},{6,7},{7,6},{8,9},{9,8},{10,11... | collective-permute-start | bytes 2359304 | tf_op jit(solution)/shard_map/ppermute | solution.py:585
  25.1 63.7 %collective-permute-start.5 = (bf16[512,768]{1,0:T(8,128)(2,1)}, bf16[512,768]{1,0:T(8,128)(2,1)}, u32[]{:S(2)}, u32[]{:S(2)}) collective-permute-start(bf16[512,768]{1,0:T(8,128)(2,1)} %get-tuple-element.132), channel_id=1, source_target_pairs={{0,2},{1,3},{2,0},{3,1},{4,6},{5,7},{6,4},{7,5},{8,10},{9,11},{10,... | collective-permute-start | bytes 2359304 | tf_op jit(solution)/shard_map/ppermute | solution.py:588
  165.1 18.7 %collective-permute-start.26 = (bf16[16,144,128]{2,1,0:T(8,128)(2,1)}, bf16[16,144,128]{2,1,0:T(8,128)(2,1)}, u32[]{:S(2)}, u32[]{:S(2)}) collective-permute-start(bf16[16,144,128]{2,1,0:T(8,128)(2,1)} %get-tuple-element.82), channel_id=1, source_target_pairs={{0,1},{1,0},{2,3},{3,2},{4,5},{5,4},{6,7},{7,6},{8,9},{9,8},{10,11... | collective-permute-start | bytes 1769480 | tf_op jit(solution)/shard_map/ppermute | solution.py:742
  165.1 21.4 %collective-permute-start.6 = (bf16[1024,384]{1,0:T(8,128)(2,1)S(1)}, bf16[1024,384]{1,0:T(8,128)(2,1)}, u32[]{:S(2)}, u32[]{:S(2)}) collective-permute-start(bf16[1024,384]{1,0:T(8,128)(2,1)S(1)} %get-tuple-element.129), channel_id=1, source_target_pairs={{0,1},{1,0},{2,3},{3,2},{4,5},{5,4},{6,7},{7,6},{8,9},{9,8},{10,11... | collective-permute-start | bytes 2359304 | tf_op jit(solution)/shard_map/ppermute | solution.py:585
  165.7 16.4 %collective-permute-start.35 = (f32[7,768]{1,0:T(8,128)S(1)}, f32[7,768]{1,0:T(8,128)S(1)}, u32[]{:S(2)}, u32[]{:S(2)}) collective-permute-start(f32[7,768]{1,0:T(8,128)S(1)} %add.671), channel_id=1, source_target_pairs={{0,16},{4,20},{8,24},{12,28},{16,0},{20,4},{24,8},{28,12},{1,17},{... | collective-permute-start | bytes 64520 | tf_op jit(solution)/shard_map/ppermute | solution.py:546
  181.5 72.2 %collective-permute-start.4 = (bf16[512,768]{1,0:T(8,128)(2,1)S(1)}, bf16[512,768]{1,0:T(8,128)(2,1)}, u32[]{:S(2)}, u32[]{:S(2)}) collective-permute-start(bf16[512,768]{1,0:T(8,128)(2,1)S(1)} %slice.79), channel_id=1, source_target_pairs={{0,2},{1,3},{2,0},{3,1},{4,6},{5,7},{6,4},{7,5},{8,10},{9,11},{10,... | collective-permute-start | bytes 2359304 | tf_op jit(solution)/shard_map/ppermute | solution.py:588
  182.1 126.3 %collective-permute-start.41 = (bf16[16,96,768]{2,1,0:T(8,128)(2,1)}, bf16[16,96,768]{2,1,0:T(8,128)(2,1)}, u32[]{:S(2)}, u32[]{:S(2)}) collective-permute-start(bf16[16,96,768]{2,1,0:T(8,128)(2,1)} %get-tuple-element.86), channel_id=1, source_target_pairs={{0,1},{1,0},{2,3},{3,2},{4,5},{5,4},{6,7},{7,6},{8,9},{9,8},{10,11... | collective-permute-start | bytes 7077896 | tf_op jit(solution)/shard_map/ppermute | solution.py:742
  182.1 129.6 %collective-permute-start.36 = (bf16[16,576,128]{2,1,0:T(8,128)(2,1)}, bf16[16,576,128]{2,1,0:T(8,128)(2,1)}, u32[]{:S(2)}, u32[]{:S(2)}) collective-permute-start(bf16[16,576,128]{2,1,0:T(8,128)(2,1)} %get-tuple-element.84), channel_id=1, source_target_pairs={{0,1},{1,0},{2,3},{3,2},{4,5},{5,4},{6,7},{7,6},{8,9},{9,8},{10,11... | collective-permute-start | bytes 7077896 | tf_op jit(solution)/shard_map/ppermute | solution.py:742
  185.0 65.5 %collective-permute-start.27 = (bf16[8,144,128]{2,1,0:T(8,128)(2,1)S(1)}, bf16[8,144,128]{2,1,0:T(8,128)(2,1)S(1)}, u32[]{:S(2)}, u32[]{:S(2)}) collective-permute-start(bf16[8,144,128]{2,1,0:T(8,128)(2,1)S(1)} %add_convert_fusion.7), channel_id=1, source_target_pairs={{0,4},{4,0},{8,12},{12,8},{16,20},{20,16},{24,28},{28,24},{1,5},{5... | collective-permute-start | bytes 884744 | tf_op jit(solution)/shard_map/ppermute | solution.py:535
  209.3 53.9 %collective-permute-start.22 = (bf16[4,96,384]{2,1,0:T(8,128)(2,1)}, bf16[4,96,384]{2,1,0:T(8,128)(2,1)}, u32[]{:S(2)}, u32[]{:S(2)}) collective-permute-start(bf16[4,96,384]{2,1,0:T(8,128)(2,1)} %get-tuple-element.80), channel_id=1, source_target_pairs={{0,4},{4,0},{8,12},{12,8},{16,20},{20,16},{24,28},{28,24},{1,5},{5... | collective-permute-start | bytes 884744 | tf_op jit(solution)/shard_map/ppermute | solution.py:742
  250.5 14.1 %collective-permute-start.19 = (bf16[4,96,384]{2,1,0:T(8,128)(2,1)}, bf16[4,96,384]{2,1,0:T(8,128)(2,1)}, u32[]{:S(2)}, u32[]{:S(2)}) collective-permute-start(bf16[4,96,384]{2,1,0:T(8,128)(2,1)} %get-tuple-element.78), channel_id=1, source_target_pairs={{0,4},{4,0},{8,12},{12,8},{16,20},{20,16},{24,28},{28,24},{1,5},{5... | collective-permute-start | bytes 884744 | tf_op jit(solution)/shard_map/ppermute | solution.py:742
  280.1 11.4 %collective-permute-start.8 = (bf16[1024,384]{1,0:T(8,128)(2,1)}, bf16[1024,384]{1,0:T(8,128)(2,1)S(1)}, u32[]{:S(2)}, u32[]{:S(2)}) collective-permute-start(bf16[1024,384]{1,0:T(8,128)(2,1)} %get-tuple-element.62.gsend_ref), channel_id=1, source_target_pairs={{0,1},{1,0},{2,3},{3,2},{4,5},{5,4},{6,7},{7,6},{8,9},{9,8},{10,11... | collective-permute-start | bytes 2359304 | tf_op jit(solution)/shard_map/ppermute | solution.py:585
  291.2 24.5 %collective-permute-start.21 = (bf16[1,96,384]{2,1,0:T(8,128)(2,1)S(1)}, bf16[1,96,384]{2,1,0:T(8,128)(2,1)S(1)}, u32[]{:S(2)}, u32[]{:S(2)}) collective-permute-start(bf16[1,96,384]{2,1,0:T(8,128)(2,1)S(1)} %add_convert_fusion.16), channel_id=1, source_target_pairs={{0,16},{4,20},{8,24},{12,28},{16,0},{20,4},{24,8},{28,12},{1,17},{... | collective-permute-start | bytes 221192 | tf_op jit(solution)/shard_map/ppermute | solution.py:535
  291.5 27.0 %collective-permute-start.18 = (bf16[1,96,384]{2,1,0:T(8,128)(2,1)S(1)}, bf16[1,96,384]{2,1,0:T(8,128)(2,1)S(1)}, u32[]{:S(2)}, u32[]{:S(2)}) collective-permute-start(bf16[1,96,384]{2,1,0:T(8,128)(2,1)S(1)} %add_convert_fusion.17), channel_id=1, source_target_pairs={{0,16},{4,20},{8,24},{12,28},{16,0},{20,4},{24,8},{28,12},{1,17},{... | collective-permute-start | bytes 221192 | tf_op jit(solution)/shard_map/ppermute | solution.py:535
  311.2 42.5 %collective-permute-start.42 = (bf16[8,96,768]{2,1,0:T(8,128)(2,1)}, bf16[8,96,768]{2,1,0:T(8,128)(2,1)}, u32[]{:S(2)}, u32[]{:S(2)}) collective-permute-start(bf16[8,96,768]{2,1,0:T(8,128)(2,1)} %add_convert_fusion.1), channel_id=1, source_target_pairs={{0,4},{4,0},{8,12},{12,8},{16,20},{20,16},{24,28},{28,24},{1,5},{5... | collective-permute-start | bytes 3538952 | tf_op jit(solution)/shard_map/ppermute | solution.py:535
  314.3 42.1 %collective-permute-start.37 = (bf16[8,576,128]{2,1,0:T(8,128)(2,1)}, bf16[8,576,128]{2,1,0:T(8,128)(2,1)}, u32[]{:S(2)}, u32[]{:S(2)}) collective-permute-start(bf16[8,576,128]{2,1,0:T(8,128)(2,1)} %add_convert_fusion.2), channel_id=1, source_target_pairs={{0,2},{1,3},{2,0},{3,1},{4,6},{5,7},{6,4},{7,5},{8,10},{9,11},{10,... | collective-permute-start | bytes 3538952 | tf_op jit(solution)/shard_map/ppermute | solution.py:535
  316.9 25.6 %collective-permute-start.12 = (f32[11,768]{1,0:T(8,128)S(1)}, f32[11,768]{1,0:T(8,128)S(1)}, u32[]{:S(2)}, u32[]{:S(2)}) collective-permute-start(f32[11,768]{1,0:T(8,128)S(1)} %fusion.29), channel_id=1, source_target_pairs={{0,2},{1,3},{2,0},{3,1},{4,6},{5,7},{6,4},{7,5},{8,10},{9,11},{10,... | collective-permute-start | bytes 101384 | tf_op jit(solution)/shard_map/ppermute | solution.py:546
  348.4 12.0 %collective-permute-start.25 = (bf16[3,96,192]{1,2,0:T(8,128)(2,1)S(1)}, bf16[3,96,192]{1,2,0:T(8,128)(2,1)S(1)}, u32[]{:S(2)}, u32[]{:S(2)}) collective-permute-start(bf16[3,96,192]{1,2,0:T(8,128)(2,1)S(1)} %fusion.6), channel_id=1, source_target_pairs={{0,2},{1,3},{2,0},{3,1},{4,6},{5,7},{6,4},{7,5},{8,10},{9,11},{10,... | collective-permute-start | bytes 331784 | tf_op jit(solution)/shard_map/ppermute | solution.py:778
  349.0 36.8 %collective-permute-start.10 = (bf16[512,768]{1,0:T(8,128)(2,1)}, bf16[512,768]{1,0:T(8,128)(2,1)}, u32[]{:S(2)}, u32[]{:S(2)}) collective-permute-start(bf16[512,768]{1,0:T(8,128)(2,1)} %get-tuple-element.65), channel_id=1, source_target_pairs={{0,2},{1,3},{2,0},{3,1},{4,6},{5,7},{6,4},{7,5},{8,10},{9,11},{10,... | collective-permute-start | bytes 2359304 | tf_op jit(solution)/shard_map/ppermute | solution.py:588
  355.9 25.0 %collective-permute-start.43 = (bf16[4,96,768]{2,1,0:T(8,128)(2,1)}, bf16[4,96,768]{2,1,0:T(8,128)(2,1)}, u32[]{:S(2)}, u32[]{:S(2)}) collective-permute-start(bf16[4,96,768]{2,1,0:T(8,128)(2,1)} %add_convert_fusion.3), channel_id=1, source_target_pairs={{0,2},{1,3},{2,0},{3,1},{4,6},{5,7},{6,4},{7,5},{8,10},{9,11},{10,... | collective-permute-start | bytes 1769480 | tf_op jit(solution)/shard_map/ppermute | solution.py:535
  358.9 25.1 %collective-permute-start.38 = (bf16[4,576,128]{2,1,0:T(8,128)(2,1)}, bf16[4,576,128]{2,1,0:T(8,128)(2,1)}, u32[]{:S(2)}, u32[]{:S(2)}) collective-permute-start(bf16[4,576,128]{2,1,0:T(8,128)(2,1)} %add_convert_fusion.4), channel_id=1, source_target_pairs={{0,4},{4,0},{8,12},{12,8},{16,20},{20,16},{24,28},{28,24},{1,5},{5... | collective-permute-start | bytes 1769480 | tf_op jit(solution)/shard_map/ppermute | solution.py:535
  382.2 15.3 %collective-permute-start.44 = (bf16[2,96,768]{2,1,0:T(8,128)(2,1)S(1)}, bf16[2,96,768]{2,1,0:T(8,128)(2,1)S(1)}, u32[]{:S(2)}, u32[]{:S(2)}) collective-permute-start(bf16[2,96,768]{2,1,0:T(8,128)(2,1)S(1)} %add_convert_fusion.5), channel_id=1, source_target_pairs={{0,8},{4,12},{8,0},{12,4},{16,24},{20,28},{24,16},{28,20},{1,9},{5... | collective-permute-start | bytes 884744 | tf_op jit(solution)/shard_map/ppermute | solution.py:535
  (65 other events, 671.5 us)

commit v2 on v1

v2 whole, which is shorter than its diff:
```python
import functools

import jax
import jax.numpy as jnp
from jax import lax
from jax.experimental import pallas as pl
from jax.experimental.pallas import tpu as pltpu
from jax.sharding import PartitionSpec as P

HEAD_DIM = 64
LANES = 128
EPSILON = 1e-05
NEGATIVE = -1000000000.0
QBLOCK = 512
KBLOCK = 256
VMEM_BYTES = 60 << 20
F32 = jnp.float32
BF16 = jnp.bfloat16

CORE = [(i, i ^ 1) for i in range(4)]
PAIR = [(i, i ^ 2) for i in range(4)]


def dot_nt(left, right):
    return lax.dot_general(left, right, (((1,), (1,)), ((), ())), preferred_element_type=F32)


def dot_nn(left, right):
    return lax.dot_general(left, right, (((1,), (0,)), ((), ())), preferred_element_type=F32)


def dot_tn(left, right):
    return lax.dot_general(left, right, (((0,), (0,)), ((), ())), preferred_element_type=F32)


def params():
    return pltpu.CompilerParams(vmem_limit_bytes=VMEM_BYTES)


def once(shape, index_map):
    return pl.BlockSpec(shape, index_map, pipeline_mode=pl.Buffered(1))


def still(array):
    return once(array.shape, lambda *_: (0,) * array.ndim)


SMEM_SPEC = pl.BlockSpec(memory_space=pltpu.SMEM)


def norm_stats(values):
    center = values - jnp.mean(values, axis=-1, keepdims=True)
    inv_std = lax.rsqrt(jnp.mean(center * center, axis=-1, keepdims=True) + EPSILON)
    return center * inv_std, inv_std


def norm_backward(grad_out, norm_gain, scaled, inv_std):
    weighted = grad_out * norm_gain
    return inv_std * (
        weighted
        - jnp.mean(weighted, axis=-1, keepdims=True)
        - scaled * jnp.mean(weighted * scaled, axis=-1, keepdims=True)
    )


def project_kernel(s_ref, x_ref, gain_ref, bias_ref, w_ref, normed_ref, proj_ref):
    tile = 128
    for first in range(0, x_ref.shape[0], tile):
        rows = slice(first, first + tile)
        scaled, _ = norm_stats(x_ref[rows, :].astype(F32))
        normed = (scaled * gain_ref[...] + bias_ref[...]).astype(BF16)
        normed_ref[:, rows] = normed.T
        proj_ref[rows, :] = dot_nn(normed, w_ref[...]).astype(BF16)


def project(scalars, x, gain, bias, weights):
    rows, width = x.shape
    cols = weights.shape[1] // 2
    return pl.pallas_call(
        project_kernel,
        grid_spec=pltpu.PrefetchScalarGridSpec(
            num_scalar_prefetch=1,
            grid=(1,),
            in_specs=[
                pl.BlockSpec((rows, width), lambda i, s: (0, 0)),
                pl.BlockSpec((1, width), lambda i, s: (0, 0)),
                pl.BlockSpec((1, width), lambda i, s: (0, 0)),
                pl.BlockSpec((width, cols), lambda i, s: (0, s[0])),
            ],
            out_specs=[
                pl.BlockSpec((width, rows), lambda i, s: (0, 0)),
                pl.BlockSpec((rows, cols), lambda i, s: (0, 0)),
            ],
        ),
        out_shape=[
            jax.ShapeDtypeStruct((width, rows), BF16),
            jax.ShapeDtypeStruct((rows, cols), BF16),
        ],
        compiler_params=params(),
        cost_estimate=pl.CostEstimate(
            flops=2 * rows * width * cols, bytes_accessed=6 * rows * width, transcendentals=0
        ),
        name="project",
    )(scalars, x, gain, bias, weights)


def store_parts(flag, parts, keep_ref, send_ref):
    first = jnp.concatenate(parts[0], axis=0)
    second = jnp.concatenate(parts[1], axis=0)
    keep = jnp.where(flag == 0, first, second)
    send = jnp.where(flag == 0, second, first)
    keep_ref[...] = keep.astype(BF16).reshape(keep_ref.shape)
    send_ref[...] = send.astype(BF16).reshape(send_ref.shape)


def lane_tiles(values):
    return [values[:, n : n + LANES] for n in range(0, values.shape[1], LANES)]


def only_head(values, head):
    lane = lax.broadcasted_iota(jnp.int32, values.shape, 1)
    return jnp.where((lane // HEAD_DIM) == head, values, jnp.zeros_like(values))


def load_natural(member, blocks, dest, size, shift=0):
    for slot, block in enumerate(blocks):
        start = pl.multiple_of(lax.bitwise_xor(member, slot) * size, 8) + shift
        start = pl.multiple_of(start, 8)
        dest[pl.ds(start, size), :] = block.astype(dest.dtype)


def attend_kernel(
    m_ref, p0, p1, p2, p3, taps_ref, mixed_ref, own_ref, send_ref, lse_ref, pj, kh, vt, on, qs
):
    member = m_ref[1]
    size = p0.shape[0]
    length = 4 * size
    scale = jnp.asarray(HEAD_DIM ** (-0.5), BF16)
    for c in range(3):
        cols = slice(c * LANES, (c + 1) * LANES)
        pj[c, 0:8, :] = jnp.zeros((8, LANES), F32)
        load_natural(member, [p[:, cols] for p in (p0, p1, p2, p3)], pj.at[c], size, 8)
    for c in range(3):
        total = taps_ref[0, 3 * c : 3 * c + 1, :] * pj[c, 8 : 8 + length, :]
        total = total + taps_ref[0, 3 * c + 1 : 3 * c + 2, :] * pj[c, 7 : 7 + length, :]
        total = total + taps_ref[0, 3 * c + 2 : 3 * c + 3, :] * pj[c, 6 : 6 + length, :]
        mixed = total.astype(BF16)
        mixed_ref[:, c * LANES : (c + 1) * LANES] = mixed
        if c == 0:
            qs[...] = mixed * scale
        elif c == 1:
            kh[0] = only_head(mixed, 0)
            kh[1] = only_head(mixed, 1)
        else:
            vt[...] = mixed.T
    for first in range(0, length, QBLOCK):
        queries = qs[first : first + QBLOCK, :]
        keys = first + QBLOCK
        outs = []
        for head in range(2):
            scores = dot_nt(kh[head, 0:keys, :], queries)
            key_pos = lax.broadcasted_iota(jnp.int32, (QBLOCK, QBLOCK), 0)
            query_pos = lax.broadcasted_iota(jnp.int32, (QBLOCK, QBLOCK), 1)
            corner = jnp.where(key_pos <= query_pos, scores[first:keys, :], NEGATIVE)
            if first:
                scores = jnp.concatenate([scores[:first, :], corner], axis=0)
            else:
                scores = corner
            top = jnp.max(scores, axis=0, keepdims=True)
            weights = jnp.exp(scores - top)
            total = jnp.sum(weights, axis=0, keepdims=True)
            part = dot_nn(
                vt[head * HEAD_DIM : (head + 1) * HEAD_DIM, 0:keys], weights.astype(BF16)
            )
            outs.append(part * (1.0 / total))
            lse_ref[0, head : head + 1, first : first + QBLOCK] = top + jnp.log(total)
        on[first : first + QBLOCK, :] = jnp.concatenate(outs, axis=0).T.astype(BF16)
    for slot in range(4):
        start = pl.multiple_of(lax.bitwise_xor(member, slot) * size, size)
        block = on[pl.ds(start, size), :]
        dest = (own_ref, send_ref)[slot % 2]
        dest[slot // 2 * size : (slot // 2 + 1) * size, :] = block


def attend(member, proj, taps):
    size = proj[0].shape[0]
    pairs = proj[0].shape[1] // (3 * LANES)
    length = 4 * size
    width = pairs * LANES
    return pl.pallas_call(
        attend_kernel,
        grid=(pairs,),
        in_specs=[SMEM_SPEC]
        + [pl.BlockSpec((size, 3 * LANES), lambda p: (0, p))] * 4
        + [pl.BlockSpec((1, 16, LANES), lambda p: (p, 0, 0))],
        out_specs=[
            pl.BlockSpec((length, 3 * LANES), lambda p: (0, p)),
            pl.BlockSpec((2 * size, LANES), lambda p: (0, p)),
            pl.BlockSpec((2 * size, LANES), lambda p: (0, p)),
            pl.BlockSpec((1, 2, length), lambda p: (p, 0, 0)),
        ],
        out_shape=[
            jax.ShapeDtypeStruct((length, 3 * width), BF16),
            jax.ShapeDtypeStruct((2 * size, width), BF16),
            jax.ShapeDtypeStruct((2 * size, width), BF16),
            jax.ShapeDtypeStruct((pairs, 2, length), F32),
        ],
        scratch_shapes=[
            pltpu.VMEM((3, 8 + length, LANES), F32),
            pltpu.VMEM((2, length, LANES), BF16),
            pltpu.VMEM((LANES, length), BF16),
            pltpu.VMEM((length, LANES), BF16),
            pltpu.VMEM((length, LANES), BF16),
        ],
        compiler_params=params(),
        cost_estimate=pl.CostEstimate(
            flops=pairs * 14 * 10**9, bytes_accessed=12 << 20, transcendentals=0
        ),
        name="attend",
    )(member, *proj, taps)


def attend_back_kernel(
    m_ref,
    p0,
    p1,
    p2,
    p3,
    mixed_ref,
    lse_ref,
    taps_ref,
    own_ref,
    send_ref,
    down_ref,
    drecv_ref,
    n0,
    n1,
    n2,
    n3,
    gown_ref,
    gsend_ref,
    gconv_ref,
    keep_ref,
    give_ref,
    pj,
    dm,
    qh,
    doh,
    kt,
    dl,
    dqa,
    nat,
    gp,
):
    member = m_ref[1]
    size = p0.shape[0]
    length = 4 * size
    scale = jnp.asarray(HEAD_DIM ** (-0.5), BF16)
    halves = [slice(0, size), slice(size, 2 * size)]
    load_natural(
        member,
        [own_ref[halves[0]], send_ref[halves[0]], own_ref[halves[1]], send_ref[halves[1]]],
        nat.at[0],
        size,
    )
    load_natural(
        member,
        [down_ref[halves[0]], drecv_ref[halves[0]], down_ref[halves[1]], drecv_ref[halves[1]]],
        nat.at[1],
        size,
    )
    grads = nat[1]
    product = (grads.astype(F32) * nat[0].astype(F32)).T
    for head in range(2):
        dl[head : head + 1, :] = jnp.sum(
            product[head * HEAD_DIM : (head + 1) * HEAD_DIM, :], axis=0, keepdims=True
        )
        doh[head] = only_head(grads, head)
        qh[head] = only_head(mixed_ref[:, 0:LANES], head) * scale
    kt[...] = mixed_ref[:, LANES : 2 * LANES].T
    for c in range(3):
        cols = slice(c * LANES, (c + 1) * LANES)
        pj[c, 0:8, :] = jnp.zeros((8, LANES), F32)
        dm[c, length : length + 8, :] = jnp.zeros((8, LANES), F32)
        load_natural(member, [p[:, cols] for p in (p0, p1, p2, p3)], pj.at[c], size, 8)
    for first in range(0, length, KBLOCK):
        keys = mixed_ref[first : first + KBLOCK, LANES : 2 * LANES]
        values = mixed_ref[first : first + KBLOCK, 2 * LANES : 3 * LANES]
        sum_v = None
        sum_k = None
        for head in range(2):
            scores = dot_nt(keys, qh[head, first:, :])
            key_pos = lax.broadcasted_iota(jnp.int32, (KBLOCK, KBLOCK), 0)
            query_pos = lax.broadcasted_iota(jnp.int32, (KBLOCK, KBLOCK), 1)
            corner = jnp.where(key_pos <= query_pos, scores[:, :KBLOCK], NEGATIVE)
            if first + KBLOCK < length:
                scores = jnp.concatenate([corner, scores[:, KBLOCK:]], axis=1)
            else:
                scores = corner
            probs = jnp.exp(scores - lse_ref[0, head : head + 1, first:])
            grad_probs = dot_nt(values, doh[head, first:, :])
            grad_scores = (probs * (grad_probs - dl[head : head + 1, first:])).astype(BF16)
            part_v = dot_nn(probs.astype(BF16), doh[head, first:, :])
            part_k = dot_nn(grad_scores, qh[head, first:, :])
            sum_v = part_v if sum_v is None else sum_v + part_v
            sum_k = part_k if sum_k is None else sum_k + part_k
            lanes = slice(head * HEAD_DIM, (head + 1) * HEAD_DIM)
            part_q = dot_nn(kt[lanes, first : first + KBLOCK], grad_scores)
            if first == 0:
                dqa[lanes, :] = part_q
            else:
                dqa[lanes, first:] += part_q
        dm[1, first : first + KBLOCK, :] = sum_k
        dm[2, first : first + KBLOCK, :] = sum_v
    dm[0, 0:length, :] = dqa[...].T * HEAD_DIM ** (-0.5)
    for c in range(3):
        grad = dm[c, 0:length, :]
        for s in range(3):
            gconv_ref[3 * c + s : 3 * c + s + 1, :] = jnp.sum(
                grad * pj[c, 8 - s : 8 - s + length, :], axis=0, keepdims=True
            )
        total = taps_ref[0, 3 * c : 3 * c + 1, :] * grad
        total = total + taps_ref[0, 3 * c + 1 : 3 * c + 2, :] * dm[c, 1 : 1 + length, :]
        total = total + taps_ref[0, 3 * c + 2 : 3 * c + 3, :] * dm[c, 2 : 2 + length, :]
        gp[:, c * LANES : (c + 1) * LANES] = total.astype(BF16)
    total = None
    for slot, norm in enumerate((n0, n1, n2, n3)):
        start = pl.multiple_of(lax.bitwise_xor(member, slot) * size, size)
        dest = (gown_ref, gsend_ref)[slot % 2]
        block = gp[pl.ds(start, size), :]
        dest[slot // 2 * size : (slot // 2 + 1) * size, :] = block
        part = dot_nn(norm[...], block)
        total = part if total is None else total + part
    rows = total.shape[0] // 8
    store_parts(
        m_ref[3],
        [
            [total[b * rows : (b + 1) * rows] for b in (x, x + 4, x + 2, x + 6)]
            for x in range(2)
        ],
        keep_ref,
        give_ref,
    )


def attend_back(pair, member, proj, mixed, lse, taps, own, send, grad_own, grad_recv, normed):
    size = proj[0].shape[0]
    length = 4 * size
    width = normed[0].shape[0]
    part = jax.ShapeDtypeStruct((2, 2, width // 8, 3 * LANES), BF16)
    half_spec = pl.BlockSpec((2 * size, LANES), lambda i: (0, pair))
    return pl.pallas_call(
        attend_back_kernel,
        grid=(1,),
        in_specs=[SMEM_SPEC]
        + [pl.BlockSpec((size, 3 * LANES), lambda i: (0, pair))] * 4
        + [
            pl.BlockSpec((length, 3 * LANES), lambda i: (0, pair)),
            pl.BlockSpec((1, 2, length), lambda i: (pair, 0, 0)),
            pl.BlockSpec((1, 16, LANES), lambda i: (pair, 0, 0)),
        ]
        + [half_spec] * 4
        + [pl.BlockSpec((width, size), lambda i: (0, 0))] * 4,
        out_specs=[
            pl.BlockSpec((2 * size, 3 * LANES), lambda i: (0, 0)),
            pl.BlockSpec((2 * size, 3 * LANES), lambda i: (0, 0)),
            pl.BlockSpec((16, LANES), lambda i: (0, 0)),
            pl.BlockSpec(part.shape, lambda i: (0, 0, 0, 0)),
            pl.BlockSpec(part.shape, lambda i: (0, 0, 0, 0)),
        ],
        out_shape=[
            jax.ShapeDtypeStruct((2 * size, 3 * LANES), BF16),
            jax.ShapeDtypeStruct((2 * size, 3 * LANES), BF16),
            jax.ShapeDtypeStruct((16, LANES), F32),
            part,
            part,
        ],
        scratch_shapes=[
            pltpu.VMEM((3, 8 + length, LANES), F32),
            pltpu.VMEM((3, 8 + length, LANES), F32),
            pltpu.VMEM((2, length, LANES), BF16),
            pltpu.VMEM((2, length, LANES), BF16),
            pltpu.VMEM((LANES, length), BF16),
            pltpu.VMEM((8, length), F32),
            pltpu.VMEM((LANES, length), F32),
            pltpu.VMEM((2, length, LANES), BF16),
            pltpu.VMEM((length, 3 * LANES), BF16),
        ],
        compiler_params=params(),
        cost_estimate=pl.CostEstimate(
            flops=12 * 10**9, bytes_accessed=12 << 20, transcendentals=0
        ),
        name="attend_back",
    )(member, *proj, mixed, lse, taps, own, send, grad_own, grad_recv, *normed)


def canonical(flag, own_ref, recv_ref):
    own = own_ref[...]
    recv = recv_ref[...]
    return jnp.concatenate(
        [jnp.where(flag == 0, own, recv), jnp.where(flag == 0, recv, own)], axis=1
    )


def ffn_forward_kernel(
    s_ref,
    hown_ref,
    hrecv_ref,
    wout_ref,
    tok0,
    tok1,
    cot0,
    cot1,
    gain_ref,
    bias_ref,
    up_ref,
    upb_ref,
    down_ref,
    downb_ref,
    res_ref,
    nf_ref,
    gf_ref,
    relu_ref,
    out0,
    out1,
    dbias_ref,
    keep_ref,
    send_ref,
    acc,
):
    step = pl.program_id(0)
    size = tok0.shape[0]
    core = s_ref[0]
    halves = ((0, s_ref[1] * size), (size, lax.bitwise_xor(s_ref[1], 2) * size))

    def valid(start):
        row = start + lax.broadcasted_iota(jnp.int32, tok0.shape, 0)
        return row < s_ref[2]

    @pl.when(step == 0)
    def _():
        attended = dot_nn(canonical(core, hown_ref, hrecv_ref), wout_ref[...])
        for tok, cot, (first, start) in zip((tok0, tok1), (cot0, cot1), halves):
            rows = slice(first, first + size)
            residual = tok[...].astype(F32) + attended[rows]
            res_ref[rows, :] = residual
            scaled, _ = norm_stats(residual)
            nf_ref[rows, :] = (scaled * gain_ref[...] + bias_ref[...]).astype(BF16)
            grad = cot[...]
            gf_ref[rows, :] = jnp.where(valid(start), grad, jnp.zeros_like(grad))
        dbias_ref[0:1, :] = jnp.sum(gf_ref[...].astype(F32), axis=0, keepdims=True)
        acc[...] = jnp.zeros_like(acc)

    relu = jnp.maximum(dot_nn(nf_ref[...], up_ref[...]) + upb_ref[...], 0.0)
    relu_ref[...] = relu
    act = (relu * relu).astype(BF16)
    acc[...] += dot_nn(act, down_ref[...])
    grad = dot_tn(act, gf_ref[...])
    rows = grad.shape[0] // 8
    store_parts(
        core,
        [
            [
                tile
                for chunk in (bit, bit + 4, bit + 2, bit + 6)
                for tile in lane_tiles(grad[chunk * rows : (chunk + 1) * rows])
            ]
            for bit in range(2)
        ],
        keep_ref,
        send_ref,
    )

    @pl.when(step == pl.num_programs(0) - 1)
    def _():
        for out, (first, start) in zip((out0, out1), halves):
            rows = slice(first, first + size)
            total = res_ref[rows, :] + (acc[rows, :] + downb_ref[...])
            out[...] = jnp.where(valid(start), total, 0.0).astype(BF16)


def ffn_forward(scalars, hown, hrecv, wout, toks, cots, gain, bias, up, upb, down, downb):
    rows = 2 * toks[0].shape[0]
    width, ff = up.shape
    tile = ff // 4
    part = jax.ShapeDtypeStruct((2, 2, 2, 2, tile // 8 * width // LANES, LANES), BF16)
    part_spec = pl.BlockSpec(
        (2, 2, 1, 1) + part.shape[4:], lambda j: (0, 0, lax.rem(j, 2), lax.div(j, 2), 0, 0)
    )
    full = lambda dtype: jax.ShapeDtypeStruct((rows, width), dtype)
    block = jax.ShapeDtypeStruct(toks[0].shape, BF16)
    return pl.pallas_call(
        ffn_forward_kernel,
        grid=(4,),
        in_specs=[SMEM_SPEC]
        + [still(a) for a in (hown, hrecv, wout, *toks, *cots, gain, bias)]
        + [
            pl.BlockSpec((width, tile), lambda j: (0, j)),
            pl.BlockSpec((1, tile), lambda j: (0, j)),
            pl.BlockSpec((tile, width), lambda j: (j, 0)),
            still(downb),
        ],
        out_specs=[once((rows, width), lambda j: (0, 0))] * 3
        + [pl.BlockSpec((rows, tile), lambda j: (0, j))]
        + [once(block.shape, lambda j: (0, 0))] * 2
        + [pl.BlockSpec((8, width), lambda j: (0, 0)), part_spec, part_spec],
        out_shape=[
            full(F32),
            full(BF16),
            full(BF16),
            jax.ShapeDtypeStruct((rows, ff), F32),
            block,
            block,
            jax.ShapeDtypeStruct((8, width), F32),
            part,
            part,
        ],
        scratch_shapes=[pltpu.VMEM((rows, width), F32)],
        compiler_params=params(),
        cost_estimate=pl.CostEstimate(
            flops=2 * rows * width * (3 * ff + width), bytes_accessed=40 << 20, transcendentals=0
        ),
        name="ffn_forward",
    )(scalars, hown, hrecv, wout, *toks, *cots, gain, bias, up, upb, down, downb)


def ffn_backward_kernel(
    s_ref,
    gf_ref,
    nf_ref,
    res_ref,
    hown_ref,
    hrecv_ref,
    wout_ref,
    gain_ref,
    relu_ref,
    up_ref,
    down_ref,
    gres_ref,
    gown_ref,
    gsend_ref,
    upb_ref,
    sums_ref,
    keep_ref,
    send_ref,
    nft,
    gn,
):
    step = pl.program_id(0)
    last = pl.num_programs(0) - 1
    core = s_ref[0]

    def store(grad):
        rows = grad.shape[0] // 32
        store_parts(
            core,
            [
                [
                    tile
                    for place in range(16)
                    for chunk in [
                        bit
                        + (place >> 3 & 1) * 2
                        + (place >> 2 & 1) * 4
                        + (place >> 1 & 1) * 8
                        + (place & 1) * 16
                    ]
                    for tile in lane_tiles(grad[chunk * rows : (chunk + 1) * rows])
                ]
                for bit in range(2)
            ],
            keep_ref,
            send_ref,
        )

    @pl.when(step == 0)
    def _():
        nft[...] = nf_ref[...].T
        gn[...] = jnp.zeros_like(gn)

    @pl.when(step < last)
    def _():
        grad_act = dot_nt(gf_ref[...], down_ref[...])
        grad_pre = (2.0 * relu_ref[...] * grad_act).astype(BF16)
        upb_ref[...] = jnp.sum(grad_pre.astype(F32), axis=0, keepdims=True)
        gn[...] += dot_nt(grad_pre, up_ref[...])
        store(dot_nn(nft[...], grad_pre))

    @pl.when(step == last)
    def _():
        scaled, inv_std = norm_stats(res_ref[...])
        grad = gn[...]
        sums_ref[0:1, :] = jnp.sum(grad * scaled, axis=0, keepdims=True)
        sums_ref[1:2, :] = jnp.sum(grad, axis=0, keepdims=True)
        total = gf_ref[...].astype(F32) + norm_backward(grad, gain_ref[...], scaled, inv_std)
        gres_ref[...] = total
        attended = total.astype(BF16)
        heads = dot_nt(attended, wout_ref[...]).astype(BF16)
        middle = heads.shape[1] // 2
        gown_ref[...] = jnp.where(core == 0, heads[:, :middle], heads[:, middle:])
        gsend_ref[...] = jnp.where(core == 0, heads[:, middle:], heads[:, :middle])
        store(dot_tn(canonical(core, hown_ref, hrecv_ref), attended))


def ffn_backward(scalars, gf, nf, res, hown, hrecv, wout, gain, relu, up, down):
    rows, width = nf.shape
    ff = up.shape[1]
    tile = ff // 4
    block = width // 32 * tile // LANES
    part = jax.ShapeDtypeStruct((2, 2, 2, 2, 5 * block, LANES), BF16)
    part_spec = pl.BlockSpec((2, 2, 2, 2, block, LANES), lambda j: (0, 0, 0, 0, j, 0))
    now = lambda j: jnp.minimum(j, 3)
    half = jax.ShapeDtypeStruct(hown.shape, BF16)
    return pl.pallas_call(
        ffn_backward_kernel,
        grid=(5,),
        in_specs=[SMEM_SPEC]
        + [still(a) for a in (gf, nf, res, hown, hrecv, wout, gain)]
        + [
            pl.BlockSpec((rows, tile), lambda j: (0, now(j))),
            pl.BlockSpec((width, tile), lambda j: (0, now(j))),
            pl.BlockSpec((tile, width), lambda j: (now(j), 0)),
        ],
        out_specs=[once((rows, width), lambda j: (0, 0))]
        + [once(half.shape, lambda j: (0, 0))] * 2
        + [
            pl.BlockSpec((1, tile), lambda j: (0, now(j))),
            pl.BlockSpec((8, width), lambda j: (0, 0)),
            part_spec,
            part_spec,
        ],
        out_shape=[
            jax.ShapeDtypeStruct((rows, width), F32),
            half,
            half,
            jax.ShapeDtypeStruct((1, ff), F32),
            jax.ShapeDtypeStruct((8, width), F32),
            part,
            part,
        ],
        scratch_shapes=[pltpu.VMEM((width, rows), BF16), pltpu.VMEM((rows, width), F32)],
        compiler_params=params(),
        cost_estimate=pl.CostEstimate(
            flops=2 * rows * width * (3 * ff + 2 * width),
            bytes_accessed=40 << 20,
            transcendentals=0,
        ),
        name="ffn_backward",
    )(scalars, gf, nf, res, hown, hrecv, wout, gain, relu, up, down)


def input_grad_kernel(
    s_ref, o0, o1, o2, r0, r1, r2, w_ref, x_ref, gres_ref, gain_ref, out_ref, sums_ref, buf
):
    cols = 3 * LANES
    for n, ref in enumerate((o0, o1, o2, r0, r1, r2)):
        side = s_ref[0] if n < 3 else 1 - s_ref[0]
        start = pl.multiple_of((side * 3 + n % 3) * cols, LANES)
        buf[:, pl.ds(start, cols)] = ref[...]
    grad = dot_nt(buf[...], w_ref[...])
    scaled, inv_std = norm_stats(x_ref[...].astype(F32))

    @pl.when(pl.program_id(0) == 0)
    def _():
        sums_ref[...] = jnp.zeros_like(sums_ref)

    sums_ref[0:1, :] += jnp.sum(grad * scaled, axis=0, keepdims=True)
    sums_ref[1:2, :] += jnp.sum(grad, axis=0, keepdims=True)
    total = gres_ref[...] + norm_backward(grad, gain_ref[...], scaled, inv_std)
    out_ref[...] = total.astype(BF16)


def input_grad(slot, scalars, owns, recvs, weights, x, grad_residual, gain):
    rows, width = x.shape
    tile = rows // 2
    part = pl.BlockSpec((tile, 3 * LANES), lambda i: (2 * slot + i, 0))
    return pl.pallas_call(
        input_grad_kernel,
        grid=(2,),
        in_specs=[SMEM_SPEC]
        + [part] * 6
        + [
            still(weights),
            pl.BlockSpec((tile, width), lambda i: (i, 0)),
            pl.BlockSpec((tile, width), lambda i: (2 * slot + i, 0)),
            still(gain),
        ],
        out_specs=[
            pl.BlockSpec((tile, width), lambda i: (i, 0)),
            pl.BlockSpec((8, width), lambda i: (0, 0)),
        ],
        out_shape=[
            jax.ShapeDtypeStruct((rows, width), BF16),
            jax.ShapeDtypeStruct((8, width), F32),
        ],
        scratch_shapes=[pltpu.VMEM((tile, weights.shape[1]), BF16)],
        compiler_params=params(),
        cost_estimate=pl.CostEstimate(
            flops=2 * rows * width * weights.shape[1], bytes_accessed=8 << 20, transcendentals=0
        ),
        name="input_grad",
    )(scalars, *owns, *recvs, weights, x, grad_residual, gain)


def piece(part, axis=None, which=None):
    array, starts = part
    starts = list(starts)
    sizes = list(array.shape)
    for n in range(4):
        if starts[n] is not None:
            sizes[n] = 1
    if axis is not None:
        starts[axis] = which if array.shape[axis] == 2 else 0
        sizes[axis] = 1
    starts = [0 if s is None else s for s in starts] + [0] * (array.ndim - 4)
    return lax.dynamic_slice(array, starts, sizes).astype(F32)


def total_of(parts, axis=None, which=None):
    total = None
    for part in parts:
        value = piece(part, axis, which)
        total = value if total is None else total + value
    return total


def halve(keep, recv, stages):
    parts = [(keep, [None] * 4), (recv, [None] * 4)]
    for dim, axis, perm, bit in stages:
        sent = total_of(parts, dim, 1 - bit).astype(BF16)
        arrived = lax.ppermute(sent, axis, perm)
        for array, starts in parts:
            starts[dim] = bit if array.shape[dim] == 2 else 0
        parts.append((arrived, [None if n == 2 else 0 for n in arrived.shape[:4]]))
    return total_of(parts)


def everyone(value, hops):
    for axis, perm in hops:
        value = value + lax.ppermute(value, axis, perm)
    return value


def ffn_plain(heads, toks, cot, valid, wout, gain, bias, up, upb, down, downb):
    residual = toks.astype(F32) + jnp.dot(heads, wout, preferred_element_type=F32)
    scaled, inv_std = norm_stats(residual)
    normed = (scaled * gain + bias).astype(BF16)
    relu = jnp.maximum(jnp.dot(normed, up, preferred_element_type=F32) + upb, 0.0)
    act = jnp.square(relu).astype(BF16)
    out = jnp.dot(act, down, preferred_element_type=F32) + downb
    result = jnp.where(valid, residual + out, 0.0).astype(BF16)
    grad_ffn = jnp.where(valid, cot, jnp.zeros_like(cot))
    grad_y = grad_ffn.astype(F32)
    grad_act = jnp.einsum("td,fd->tf", grad_ffn, down, preferred_element_type=F32)
    grad_pre = (2.0 * relu * grad_act).astype(BF16)
    grad = jnp.einsum("tf,df->td", grad_pre, up, preferred_element_type=F32)
    sums = jnp.stack([jnp.sum(grad * scaled, axis=0), jnp.sum(grad, axis=0)])
    grad_residual = grad_y + norm_backward(grad, gain, scaled, inv_std)
    attended = grad_residual.astype(BF16)
    grad_heads = jnp.einsum("td,ed->te", attended, wout, preferred_element_type=F32)
    return (
        result,
        grad_residual,
        grad_heads.astype(BF16),
        sums,
        jnp.sum(grad_pre.astype(F32), axis=0),
        jnp.sum(grad_y, axis=0),
        jnp.einsum("td,tf->df", normed, grad_pre, preferred_element_type=F32),
        jnp.einsum("tf,td->fd", act, grad_ffn, preferred_element_type=F32),
        jnp.einsum("te,td->ed", heads, attended, preferred_element_type=F32),
    )


def on_device(
    tokens,
    cotangent,
    lengths,
    pre_attn_gain,
    pre_attn_bias,
    qkv_weight,
    conv_weight,
    out_weight,
    pre_ffn_gain,
    pre_ffn_bias,
    up_weight,
    up_bias,
    down_weight,
    down_bias,
):
    groups = lax.axis_size("mp")
    batch_groups = lax.axis_size("batch")
    devices = groups * batch_groups
    member = lax.axis_index("mp")
    batch = lax.axis_index("batch")
    seqs, rows, width = tokens.shape
    ff = up_weight.shape[1]
    middle = width // 2
    quarter = width // groups
    pairs = middle // LANES
    taps = conv_weight.shape[1]
    assert groups == 4 and seqs == 2 and pairs == 3 and taps == 3
    fast = batch_groups == 8 and (width // devices) % 8 == 0
    half = member // 2
    core = member % 2
    gain_attn = pre_attn_gain.astype(F32).reshape(1, width)
    bias_attn = pre_attn_bias.astype(F32).reshape(1, width)
    gain_ffn = pre_ffn_gain.astype(F32).reshape(1, width)
    bias_ffn = pre_ffn_bias.astype(F32).reshape(1, width)
    up_bias_f = up_bias.astype(F32).reshape(1, ff)
    down_bias_f = down_bias.astype(F32).reshape(1, width)

    def swap_core(value):
        return lax.ppermute(value, "mp", CORE)

    def swap_pair(value):
        return lax.ppermute(value, "mp", PAIR)

    def pick(value, index):
        return lax.dynamic_index_in_dim(value, index, 0, keepdims=False)

    length = pick(lengths, half)
    scalars = jnp.stack([core, member, length, batch % 2]).astype(jnp.int32)

    tok_pair = swap_pair(pick(tokens, 1 - half))
    tok_own = pick(tokens, half)
    cot_own = pick(cotangent, half)
    tok_core = swap_core(tok_own)
    weights = qkv_weight.reshape(3, width, 2 * pairs, LANES).transpose(1, 2, 0, 3)
    weights = weights.reshape(width, 3 * width)
    taps_own = lax.dynamic_slice_in_dim(conv_weight, core * middle, middle, 2).astype(F32)
    taps_own = taps_own.reshape(3 * taps, pairs, LANES).transpose(1, 0, 2)
    taps_own = jnp.pad(taps_own, ((0, 0), (0, 16 - 3 * taps), (0, 0)))

    def norm_project(block):
        return project(scalars, block, gain_attn, bias_attn, weights)

    first = norm_project(tok_own)
    second = norm_project(tok_core)
    tok_pair, first, second = lax.optimization_barrier((tok_pair, first, second))
    tok_cross = swap_core(tok_pair)
    cot_send, tok_late = lax.optimization_barrier((pick(cotangent, 1 - half), tok_pair))
    cot_pair = swap_pair(cot_send)
    normed, proj = zip(first, second, norm_project(tok_late), norm_project(tok_cross))
    mixed, heads_own, heads_send, lse = attend(scalars, proj, taps_own)
    heads_recv = swap_core(heads_send)

    if fast:
        (
            residual,
            normed_ffn,
            grad_ffn,
            relu,
            result_own,
            result_give,
            sums_down,
            *grads_down,
        ) = ffn_forward(
            scalars,
            heads_own,
            heads_recv,
            out_weight,
            (tok_own, tok_pair),
            (cot_own, cot_pair),
            gain_ffn,
            bias_ffn,
            up_weight,
            up_bias_f,
            down_weight,
            down_bias_f,
        )
        (
            grad_residual,
            grad_own,
            grad_send,
            sums_up,
            sums_ffn,
            *grads_up,
        ) = ffn_backward(
            scalars,
            grad_ffn,
            normed_ffn,
            residual,
            heads_own,
            heads_recv,
            out_weight,
            gain_ffn,
            relu,
            up_weight,
            down_weight,
        )
        sums_up = sums_up.reshape(ff)
        sums_down = sums_down[0]
        sums_ffn = sums_ffn[0:2]
    else:
        row = jnp.arange(rows, dtype=jnp.int32)
        row_pos = [member * rows + row, jnp.bitwise_xor(member, 2) * rows + row]
        heads_all = jnp.concatenate(
            [
                jnp.where(core == 0, heads_own, heads_recv),
                jnp.where(core == 0, heads_recv, heads_own),
            ],
            axis=1,
        )
        (
            result,
            grad_residual,
            grad_heads,
            sums_ffn,
            sums_up,
            sums_down,
            grad_up,
            grad_down,
            grad_out,
        ) = ffn_plain(
            heads_all,
            jnp.concatenate([tok_own, tok_pair], axis=0),
            jnp.concatenate([cot_own, cot_pair], axis=0),
            (jnp.concatenate(row_pos) < length)[:, None],
            out_weight,
            gain_ffn,
            bias_ffn,
            up_weight,
            up_bias_f,
            down_weight,
            down_bias_f,
        )
        result_own, result_give = result[:rows], result[rows:]
        grad_own = lax.dynamic_slice_in_dim(grad_heads, core * middle, middle, 1)
        grad_send = lax.dynamic_slice_in_dim(grad_heads, (1 - core) * middle, middle, 1)
    grad_recv = swap_core(grad_send)
    result_back = swap_pair(result_give)

    g_own, g_send, g_recv, g_conv, g_qkv = [], [], [], [], []
    for pair in range(pairs):
        own, send, conv, *grads = attend_back(
            pair,
            scalars,
            proj,
            mixed,
            lse,
            taps_own,
            heads_own,
            heads_send,
            grad_own,
            grad_recv,
            normed,
        )
        g_own.append(own)
        g_send.append(send)
        g_recv.append(swap_core(send))
        g_conv.append(conv)
        g_qkv.append(grads)
    grad_in_pair, sums_pair = input_grad(
        1, scalars, g_own, g_recv, weights, tok_pair, grad_residual, gain_attn
    )
    grad_in_back = swap_pair(grad_in_pair)
    grad_in_own, sums_own = input_grad(
        0, scalars, g_own, g_recv, weights, tok_own, grad_residual, gain_attn
    )

    def both(first, second):
        return jnp.stack([jnp.where(half == 0, first, second), jnp.where(half == 0, second, first)])

    result_all = both(result_own, result_back)
    tokens_grad = both(grad_in_own, grad_in_back)

    conv_own = jnp.stack(g_conv)[:, : 3 * taps].transpose(1, 0, 2).reshape(3 * taps, middle)
    conv_full = lax.dynamic_update_slice_in_dim(
        jnp.zeros((3 * taps, width), F32), conv_own, core * middle, 1
    )
    small = jnp.concatenate(
        [
            sums_up.reshape(ff // width, width),
            sums_down[None],
            sums_ffn,
            sums_pair[0:2] + sums_own[0:2],
            conv_full,
        ],
        axis=0,
    )
    index = batch * groups + member
    share = width // devices
    part = width // batch_groups

    if not fast:
        axes = ("batch", "mp")
        grad_qkv = 0.0
        for n, (norm, slot) in enumerate(zip(normed, (0, 0, 1, 1))):
            source = (g_own, g_send)[n % 2]
            grads = jnp.concatenate([g[slot * rows : (slot + 1) * rows] for g in source], axis=1)
            grad_qkv = grad_qkv + jnp.einsum("dt,te->de", norm, grads, preferred_element_type=F32)
        grad_qkv = grad_qkv.reshape(width, pairs, 3, LANES).transpose(2, 0, 1, 3)
        qkv_full = lax.dynamic_update_slice_in_dim(
            jnp.zeros((3, width, width), F32), grad_qkv.reshape(3, width, middle), core * middle, 2
        )
        qkv_flat = qkv_full.reshape(3, batch_groups, part, groups, quarter)
        qkv_flat = qkv_flat.transpose(1, 3, 0, 2, 4).reshape(devices * 3 * part, quarter)

        def scatter(value):
            return lax.psum_scatter(value, axes, scatter_dimension=0, tiled=True)

        small = lax.psum(small, axes)
        qkv_out = scatter(qkv_flat).reshape(3, part, quarter)
        up_out, down_out, out_out = scatter(grad_up), scatter(grad_down), scatter(grad_out)
    else:
        core_hop = ("mp", CORE)
        pair_hop = ("mp", PAIR)
        x_hop, z0_hop, z1_hop = [
            ("batch", [(i, i ^ flip) for i in range(batch_groups)]) for flip in (1, 2, 4)
        ]
        pair_stage = (0,) + pair_hop + (half,)
        x_stage = (1,) + x_hop + (batch % 2,)
        z0_stage = (2,) + z0_hop + (batch // 2 % 2,)
        z1_stage = (3,) + z1_hop + (batch // 4,)
        keep, send = grads_down
        down_sum = halve(keep, swap_core(send), [x_stage, pair_stage, z0_stage, z1_stage])
        down_out = down_sum.reshape(width // LANES, ff // devices, LANES).transpose(1, 0, 2)
        down_out = down_out.reshape(ff // devices, width)
        keep, send = grads_up
        up_sum = halve(keep, swap_core(send), [pair_stage, x_stage, z0_stage, z1_stage])
        up_sum = up_sum.reshape(-1, share, LANES)
        up_out = up_sum[: ff // LANES].transpose(1, 0, 2).reshape(share, ff)
        out_out = up_sum[ff // LANES :].transpose(1, 0, 2).reshape(share, width)
        qkv_parts = []
        for keep, send in g_qkv:
            keep = keep.reshape((1, 1) + keep.shape)
            recv = lax.ppermute(send, *x_hop).reshape(keep.shape)
            total = halve(keep, recv, [z0_stage, z1_stage])
            qkv_parts.append(total.reshape(part, 3, LANES))
        qkv_all = jnp.stack(qkv_parts, axis=1).transpose(2, 0, 1, 3)
        qkv_all = qkv_all.reshape(3, part, 2, quarter)
        lower = qkv_all[:, :, 0]
        upper = qkv_all[:, :, 1]
        keep = jnp.where(core == 0, lower, upper)
        straight = lax.ppermute(
            jnp.where(half == 0, upper, lower).astype(BF16), "mp", [(2, 0), (0, 1), (3, 2), (1, 3)]
        )
        crossed = lax.ppermute(
            jnp.where(half == 0, lower, upper).astype(BF16), "mp", [(2, 1), (1, 2)]
        )
        qkv_out = straight.astype(F32) + jnp.where(half == core, keep, crossed.astype(F32))
        small = everyone(small, [core_hop, pair_hop, x_hop, z0_hop, z1_hop])

    lead = ff // width
    mine = small[lead:]
    mine = pick(mine.reshape(mine.shape[0], devices, share).transpose(1, 0, 2), index)
    return (
        result_all,
        tokens_grad,
        mine[3],
        mine[4],
        qkv_out,
        mine[5:].reshape(3, taps, share),
        out_out,
        mine[1],
        mine[2],
        up_out,
        pick(small[:lead].reshape(devices, ff // devices), index),
        down_out,
        mine[0],
    )


def solution(mesh):
    in_specs = (
        P("batch", "mp", None),
        P("batch", "mp", None),
        P("batch"),
    ) + (P(),) * 11
    out_specs = (
        P("batch", "mp", None),
        P("batch", "mp", None),
        P(("batch", "mp")),
        P(("batch", "mp")),
        P(None, "batch", "mp"),
        P(None, None, ("batch", "mp")),
        P(("batch", "mp"), None),
        P(("batch", "mp")),
        P(("batch", "mp")),
        P(("batch", "mp"), None),
        P(("batch", "mp")),
        P(("batch", "mp"), None),
        P(("batch", "mp")),
    )
    return jax.shard_map(
        on_device, mesh=mesh, in_specs=in_specs, out_specs=out_specs, check_vma=False
    )
```

time: 415 us -> 351 us (0.85)
  matrix products: 43.8 us -> 0 us
  Pallas kernels: 154 us -> 178 us
  other arithmetic: 50.8 us -> 28.2 us
  waiting for transfers between devices: 87 us -> 64.5 us
  local copies, waits for them, and re-layouts: 29.2 us -> 36.6 us
  starting transfers between devices: 41.8 us -> 34.6 us
    dot_general x6 -> x0, matrix products: 43.8 us -> none  [the longest x1 10.2 us: on_device(): jnp.einsum('td,fd->tf', grad_ffn, down_weight, preferred_element_type=F32)]
    pallas_call x12 -> x8, Pallas kernels: 74.4 us -> 92.6 us  [the longest x1 30.1 us: ffn_backward(): pl.pallas_call(ffn_backward_kernel, grid=(5,), in_specs=[SMEM_SPEC] + [st...]
    convert_element_type x24 -> x16, other arithmetic: 29.3 us -> 15.3 us  [the longest x14 15.2 us: halve(): sent = total_of(parts, dim, 1 - bit).astype(BF16)]
    ppermute x4, waiting for transfers between devices: 17.6 us -> 8.49 us  [swap_pair(): return lax.ppermute(value, 'mp', PAIR)]
    ppermute x25 -> x19, waiting for transfers between devices: 38.4 us -> 29.5 us  [the longest x14 25.7 us: halve(): arrived = lax.ppermute(sent, axis, perm)]
    dynamic_slice x6 -> x2, local copies, waits for them, and re-layouts: 8.79 us -> 0.6 us  [pick(): return lax.dynamic_index_in_dim(value, index, 0, keepdims=False)]
    unnamed x88 -> x78, local copies, waits for them, and re-layouts: 6.24 us -> 13.3 us
    reshape x9 -> x11, local copies, waits for them, and re-layouts: 2.76 us -> 9.37 us  [the longest x1 5.84 us: on_device(): weights = weights.reshape(width, 3 * width)]
  transfers between devices with their start and end apart: 46 -> 37, of which waited for: 14 -> 14; matrix products, arithmetic and copies ran while one was open for 17% -> 16% of each run, Pallas kernels for 35% -> 35%
where the time goes in v2:
time: 351 us; the launch traced here: 344 us
  Pallas kernels  178 us (51%)
  waiting for transfers between devices  64.5 us (18%)
  local copies, waits for them, and re-layouts  36.6 us (10%)
  starting transfers between devices  34.6 us (10%)
  other arithmetic  28.2 us (8%)
    pallas_call x3, Pallas kernels, attend_back(): pl.pallas_call(attend_back_kernel, grid=(1,), in_specs=[SMEM_SPEC] + [pl....  59.3 us
    pallas_call x1, Pallas kernels, ffn_backward(): pl.pallas_call(ffn_backward_kernel, grid=(5,), in_specs=[SMEM_SPEC] + [st...  30.1 us
    pallas_call x1, Pallas kernels, ffn_forward(): pl.pallas_call(ffn_forward_kernel, grid=(4,), in_specs=[SMEM_SPEC] + [sti...  27.3 us
    pallas_call x1, Pallas kernels, attend(): pl.pallas_call(attend_kernel, grid=(pairs,), in_specs=[SMEM_SPEC] + [pl.B...  26.5 us
    ppermute x5, waiting for transfers between devices, everyone(): value = value + lax.ppermute(value, axis, perm)  26.4 us
    ppermute x14, waiting for transfers between devices, halve(): arrived = lax.ppermute(sent, axis, perm)  25.7 us
    pallas_call x4, Pallas kernels, project(): pl.pallas_call(project_kernel, grid_spec=pltpu.PrefetchScalarGridSpec(num...  20.9 us
    ppermute x14, starting transfers between devices, halve(): arrived = lax.ppermute(sent, axis, perm)  15.7 us
  transfers between devices with their start and end apart: 37, of which 14 were waited for; matrix products, arithmetic and copies ran while one was open for 16% of the time, Pallas kernels for 35%

profile of v2, /device:TPU:0, one launch (start us, length us, event | category | flops | bytes accessed | tf_op | source)
XLA Modules:
  0.0 343.8 jit_solution(6408749067914414633)
XLA Ops:
  6.6 6.1 %copy.51 = bf16[3,768,768]{1,2,0:T(8,128)(2,1)} copy(bf16[3,768,768]{2,1,0:T(8,128)(2,1)} %param.19) | data formatting | bytes 7077888 | tf_op args[5]
  12.7 4.1 %copy.52 = bf16[768,6,3,128]{0,3,2,1:T(8,128)(2,1)} copy(bf16[768,6,3,128]{0,3,1,2:T(8,128)(2,1)} %bitcast.142) | data formatting | bytes 7077888 | tf_op jit(solution)/shard_map/transpose | solution.py:828
  16.8 5.8 %copy.53.w_ref = bf16[768,2304]{1,0:T(8,128)(2,1)} copy(bf16[768,2304]{0,1:T(8,128)(2,1)} %bitcast.141) | data formatting | bytes 7077888 | tf_op jit(solution)/shard_map/reshape | solution.py:829
  25.0 5.2 %project.4 = (bf16[768,512]{1,0:T(8,128)(2,1)}, bf16[512,1152]{1,0:T(8,128)(2,1)}) custom-call(s32[4]{0:T(128)} %pad_add_fusion.s_ref.m_ref, bf16[512,768]{1,0:T(8,128)(2,1)} %copy-done.2, f32[1,768]{1,0:T(1,128)} %reshape.460.gain_ref, f32[1,768]{1,0:T(1,128)} %reshape.462.bias_ref, bf16[768,2304]{1,0:T(8,128)(2,1)} %copy.53.w_ref), custom_call_target="tpu_custom_call" | custom-call | flops 905969664 | bytes 2359296 | tf_op jit(solution)/shard_map/project/pallas_call | solution.py:79
  30.2 5.3 %project.5 = (bf16[768,512]{1,0:T(8,128)(2,1)}, bf16[512,1152]{1,0:T(8,128)(2,1)}) custom-call(s32[4]{0:T(128)} %pad_add_fusion.s_ref.m_ref, bf16[512,768]{1,0:T(8,128)(2,1)} %collective-permute-done.1.x_ref, f32[1,768]{1,0:T(1,128)} %reshape.460.gain_ref, f32[1,768]{1,0:T(1,128)} %reshape.462.bias_ref, bf16[768,2304]{1,0:T(8,128)(2,1)} %copy.53.w_ref), custom_call_target="tpu_custom_call" | custom-call | flops 905969664 | bytes 2359296 | tf_op jit(solution)/shard_map/project/pallas_call | solution.py:79
  37.9 5.2 %project.6 = (bf16[768,512]{1,0:T(8,128)(2,1)}, bf16[512,1152]{1,0:T(8,128)(2,1)}) custom-call(s32[4]{0:T(128)} %pad_add_fusion.s_ref.m_ref, bf16[512,768]{1,0:T(8,128)(2,1)} %copy-done.3, f32[1,768]{1,0:T(1,128)} %reshape.460.gain_ref, f32[1,768]{1,0:T(1,128)} %reshape.462.bias_ref, bf16[768,2304]{1,0:T(8,128)(2,1)} %copy.53.w_ref), custom_call_target="tpu_custom_call" | custom-call | flops 905969664 | bytes 2359296 | tf_op jit(solution)/shard_map/project/pallas_call | solution.py:79
  44.1 5.2 %project.7 = (bf16[768,512]{1,0:T(8,128)(2,1)}, bf16[512,1152]{1,0:T(8,128)(2,1)}) custom-call(s32[4]{0:T(128)} %pad_add_fusion.s_ref.m_ref, bf16[512,768]{1,0:T(8,128)(2,1)} %copy-done.9, f32[1,768]{1,0:T(1,128)} %reshape.460.gain_ref, f32[1,768]{1,0:T(1,128)} %reshape.462.bias_ref, bf16[768,2304]{1,0:T(8,128)(2,1)} %copy.53.w_ref), custom_call_target="tpu_custom_call" | custom-call | flops 905969664 | bytes 2359296 | tf_op jit(solution)/shard_map/project/pallas_call | solution.py:79
  49.3 26.5 %attend.1 = (bf16[2048,1152]{1,0:T(8,128)(2,1)}, bf16[1024,384]{1,0:T(8,128)(2,1)}, bf16[1024,384]{1,0:T(8,128)(2,1)}, f32[3,2,2048]{2,1,0:T(2,128)}) custom-call(s32[4]{0:T(128)} %pad_add_fusion.s_ref.m_ref, bf16[512,1152]{1,0:T(8,128)(2,1)} %get-tuple-element.71.p0, bf16[512,1152]{1,0:T(8,128)(2,1)} %get-tuple-element.72.p1, ...), custom_call_target="tpu_custom_call" | custom-call | flops 41999998976 | bytes 12582912 | tf_op jit(solution)/shard_map/attend/pallas_call | solution.py:190
  79.4 27.3 %ffn_forward.1 = (f32[1024,768]{1,0:T(8,128)}, bf16[1024,768]{1,0:T(8,128)(2,1)}, bf16[1024,768]{1,0:T(8,128)(2,1)}, f32[1024,3072]{1,0:T(8,128)}, bf16[512,768]...) custom-call(s32[4]{0:T(128)} %pad_add_fusion.s_ref.m_ref, ...), custom_call_target="tpu_custom_call" | custom-call | flops 15703474176 | bytes 41943040 | tf_op jit(solution)/shard_map/ffn_forward/pallas_call | solution.py:492
  106.7 30.1 %ffn_backward.1 = (f32[1024,768]{1,0:T(8,128)}, bf16[1024,384]{1,0:T(8,128)(2,1)}, bf16[1024,384]{1,0:T(8,128)(2,1)}, f32[1,3072]{1,0:T(1,128)}, f32[8,768]{1,0:...) custom-call(s32[4]{0:T(128)} %pad_add_fusion.s_ref.m_ref, ...), custom_call_target="tpu_custom_call" | custom-call | flops 16911433728 | bytes 41943040 | tf_op jit(solution)/shard_map/ffn_backward/pallas_call | solution.py:614
  144.5 19.7 %attend_back.3 = (bf16[1024,384]{1,0:T(8,128)(2,1)}, bf16[1024,384]{1,0:T(8,128)(2,1)}, f32[16,128]{1,0:T(8,128)}, bf16[2,2,96,384]{3,2,1,0:T(8,128)(2,1)}, bf16[2,2,96,384]{3,2,1,0:T(8,128)(2,1)}) custom-call(s32[4]{0:T(128)} %pad_add_fusion.s_ref.m_ref, bf16[512,1152]{1,0:T(8,128)(2,1)} %get-tuple-element.71.p0, bf16[512,1152]{1,0:T(8,128)(2,1)} %get-tuple-element.72.p1, ...), custom_call_target="tpu_custom_call" | custom-call | flops 12000000000 | bytes 12582912 | tf_op jit(solution)/shard_map/attend_back/pallas_call | solution.py:352
  165.6 19.9 %attend_back.4 = (bf16[1024,384]{1,0:T(8,128)(2,1)}, bf16[1024,384]{1,0:T(8,128)(2,1)}, f32[16,128]{1,0:T(8,128)}, bf16[2,2,96,384]{3,2,1,0:T(8,128)(2,1)}, bf16[2,2,96,384]{3,2,1,0:T(8,128)(2,1)}) custom-call(s32[4]{0:T(128)} %pad_add_fusion.s_ref.m_ref, bf16[512,1152]{1,0:T(8,128)(2,1)} %get-tuple-element.71.p0, bf16[512,1152]{1,0:T(8,128)(2,1)} %get-tuple-element.72.p1, ...), custom_call_target="tpu_custom_call" | custom-call | flops 12000000000 | bytes 12582912 | tf_op jit(solution)/shard_map/attend_back/pallas_call | solution.py:352
  186.1 19.7 %attend_back.5 = (bf16[1024,384]{1,0:T(8,128)(2,1)}, bf16[1024,384]{1,0:T(8,128)(2,1)}, f32[16,128]{1,0:T(8,128)}, bf16[2,2,96,384]{3,2,1,0:T(8,128)(2,1)}, bf16[2,2,96,384]{3,2,1,0:T(8,128)(2,1)}) custom-call(s32[4]{0:T(128)} %pad_add_fusion.s_ref.m_ref, bf16[512,1152]{1,0:T(8,128)(2,1)} %get-tuple-element.71.p0, bf16[512,1152]{1,0:T(8,128)(2,1)} %get-tuple-element.72.p1, ...), custom_call_target="tpu_custom_call" | custom-call | flops 12000000000 | bytes 12582912 | tf_op jit(solution)/shard_map/attend_back/pallas_call | solution.py:352
  210.6 3.7 %collective-permute-done.22 = bf16[2,2,96,384]{3,2,1,0:T(8,128)(2,1)S(1)} collective-permute-done((bf16[2,2,96,384]{3,2,1,0:T(8,128)(2,1)}, bf16[2,2,96,384]{3,2,1,0:T(8,128)(2,1)S(1)}, u32[]{:S(2)}, u32[]{:S(2)}) %collective-permute-start.22) | collective-permute-done | bytes 294944 | tf_op jit(solution)/shard_map/ppermute | solution.py:1027
  216.1 2.7 collective-permute-start.18
  220.6 2.7 collective-permute-done.18
  230.9 7.0 %input_grad.3 = (bf16[512,768]{1,0:T(8,128)(2,1)}, f32[8,768]{1,0:T(8,128)}) custom-call(s32[4]{0:T(128)} %pad_add_fusion.s_ref.m_ref, bf16[1024,384]{1,0:T(8,128)(2,1)} %get-tuple-element.94.o0, bf16[1024,384]{1,0:T(8,128)(2,1)} %get-tuple-element.95.o1, bf16[1024,384]{1,0:T(8,128)(2,1)} %get-tuple-element.96.o2, bf16[1024,384]{1,0:T(8,128)(2,1)} %copy-done.6, ...), custom_call_target="tpu_custom_call" | custom-call | flops 1811939328 | bytes 8388608 | tf_op jit(solution)/shard_map/input_grad/pallas_call | solution.py:677
  240.8 2.6 add_convert_fusion.1
  244.3 7.2 %input_grad.2 = (bf16[512,768]{1,0:T(8,128)(2,1)}, f32[8,768]{1,0:T(8,128)}) custom-call(s32[4]{0:T(128)} %pad_add_fusion.s_ref.m_ref, bf16[1024,384]{1,0:T(8,128)(2,1)} %get-tuple-element.94.o0, bf16[1024,384]{1,0:T(8,128)(2,1)} %get-tuple-element.95.o1, bf16[1024,384]{1,0:T(8,128)(2,1)} %get-tuple-element.96.o2, bf16[1024,384]{1,0:T(8,128)(2,1)} %copy-done.6, ...), custom_call_target="tpu_custom_call" | custom-call | flops 1811939328 | bytes 8388608 | tf_op jit(solution)/shard_map/input_grad/pallas_call | solution.py:677
  255.8 20.7 %collective-permute-done.12 = f32[18,768]{1,0:T(8,128)S(1)} collective-permute-done((f32[18,768]{1,0:T(8,128)S(1)}, f32[18,768]{1,0:T(8,128)S(1)}, u32[]{:S(2)}, u32[]{:S(2)}) %collective-permute-start.12) | collective-permute-done | bytes 55328 | tf_op jit(solution)/shard_map/ppermute | solution.py:740
  277.5 3.6 %collective-permute-done.13 = f32[18,768]{1,0:T(8,128)S(1)} collective-permute-done((f32[18,768]{1,0:T(8,128)S(1)}, f32[18,768]{1,0:T(8,128)S(1)}, u32[]{:S(2)}, u32[]{:S(2)}) %collective-permute-start.13) | collective-permute-done | bytes 55328 | tf_op jit(solution)/shard_map/ppermute | solution.py:740
  298.1 8.8 %collective-permute-done.34 = bf16[1,1,2,2,576,128]{5,4,3,2,1,0:T(8,128)(2,1)S(1)} collective-permute-done((bf16[1,1,2,2,576,128]{5,4,3,2,1,0:T(8,128)(2,1)}, bf16[1,1,2,2,576,128]{5,4,3,2,1,0:T(8,128)(2,1)S(1)}, u32[]{:S(2)}, u32[]{:S(2)}) %collective-permute-start.34) | collective-permute-done | bytes 589856 | tf_op jit(solution)/shard_map/ppermute | solution.py:731
  313.8 8.5 %collective-permute-done.10 = bf16[512,768]{1,0:T(8,128)(2,1)S(1)} collective-permute-done((bf16[512,768]{1,0:T(8,128)(2,1)}, bf16[512,768]{1,0:T(8,128)(2,1)S(1)}, u32[]{:S(2)}, u32[]{:S(2)}) %collective-permute-start.10) | collective-permute-done | bytes 786464 | tf_op jit(solution)/shard_map/ppermute | solution.py:816
  329.2 9.1 %collective-permute-done.36 = bf16[1,1,1,1,576,128]{5,4,3,2,1,0:T(8,128)(2,1)S(1)} collective-permute-done((bf16[1,1,1,1,576,128]{5,4,3,2,1,0:T(8,128)(2,1)S(1)}, bf16[1,1,1,1,576,128]{5,4,3,2,1,0:T(8,128)(2,1)S(1)}, u32[]{:S(2)}, u32[]{:S(2)}) %collective-permute-start.36) | collective-permute-done | bytes 147488 | tf_op jit(solution)/shard_map/ppermute | solution.py:731
  (217 shorter events, 85.6 us)
Async XLA Ops:
  3.1 27.1 %collective-permute-start.1 = (bf16[512,768]{1,0:T(8,128)(2,1)S(1)}, bf16[512,768]{1,0:T(8,128)(2,1)}, u32[]{:S(2)}, u32[]{:S(2)}) collective-permute-start(bf16[512,768]{1,0:T(8,128)(2,1)S(1)} %get-tuple-element.153.x_ref.tok0), channel_id=1, source_target_pairs={{0,1},{1,0},{2,3},{3,2},{4,5},{5,4},{6,7},{7,6},{8,9},{9,8},{10,11... | collective-permute-start | bytes 2359304 | tf_op jit(solution)/shard_map/ppermute | solution.py:813
  3.5 32.0 %collective-permute-start = (bf16[512,768]{1,0:T(8,128)(2,1)}, bf16[512,768]{1,0:T(8,128)(2,1)S(1)}, u32[]{:S(2)}, u32[]{:S(2)}) collective-permute-start(bf16[512,768]{1,0:T(8,128)(2,1)} %get-tuple-element.154), channel_id=1, source_target_pairs={{0,2},{1,3},{2,0},{3,1},{4,6},{5,7},{6,4},{7,5},{8,10},{9,11},{10,... | collective-permute-start | bytes 2359304 | tf_op jit(solution)/shard_map/ppermute | solution.py:816
  37.6 40.6 %collective-permute-start.4 = (bf16[512,768]{1,0:T(8,128)(2,1)}, bf16[512,768]{1,0:T(8,128)(2,1)S(1)}, u32[]{:S(2)}, u32[]{:S(2)}) collective-permute-start(bf16[512,768]{1,0:T(8,128)(2,1)} %get-tuple-element.79), channel_id=1, source_target_pairs={{0,2},{1,3},{2,0},{3,1},{4,6},{5,7},{6,4},{7,5},{8,10},{9,11},{10,... | collective-permute-start | bytes 2359304 | tf_op jit(solution)/shard_map/ppermute | solution.py:816
  137.3 103.5 %collective-permute-start.32 = (bf16[2,2,2,2,576,128]{5,4,3,2,1,0:T(8,128)(2,1)}, bf16[2,2,2,2,576,128]{5,4,3,2,1,0:T(8,128)(2,1)}, u32[]{:S(2)}, u32[]{:S(2)}) collective-permute-start(bf16[2,2,2,2,576,128]{5,4,3,2,1,0:T(8,128)(2,1)} %get-tuple-element.120), channel_id=1, source_target_pairs={{0,1},{1,0},{2,3},{3,2},{4,5},{5,4},{6,7},{7,6},{8,9},{9,8},{10,11... | collective-permute-start | bytes 7077896 | tf_op jit(solution)/shard_map/ppermute | solution.py:813
  137.5 100.4 %collective-permute-start.27 = (bf16[2,2,2,2,720,128]{5,4,3,2,1,0:T(8,128)(2,1)}, bf16[2,2,2,2,720,128]{5,4,3,2,1,0:T(8,128)(2,1)}, u32[]{:S(2)}, u32[]{:S(2)}) collective-permute-start(bf16[2,2,2,2,720,128]{5,4,3,2,1,0:T(8,128)(2,1)} %get-tuple-element.118), channel_id=1, source_target_pairs={{0,1},{1,0},{2,3},{3,2},{4,5},{5,4},{6,7},{7,6},{8,9},{9,8},{10,11... | collective-permute-start | bytes 8847368 | tf_op jit(solution)/shard_map/ppermute | solution.py:813
  141.8 64.0 %collective-permute-start.5 = (bf16[512,768]{1,0:T(8,128)(2,1)S(1)}, bf16[512,768]{1,0:T(8,128)(2,1)S(1)}, u32[]{:S(2)}, u32[]{:S(2)}) collective-permute-start(bf16[512,768]{1,0:T(8,128)(2,1)S(1)} %copy-done.28), channel_id=1, source_target_pairs={{0,2},{1,3},{2,0},{3,1},{4,6},{5,7},{6,4},{7,5},{8,10},{9,11},{10,... | collective-permute-start | bytes 2359304 | tf_op jit(solution)/shard_map/ppermute | solution.py:816
  164.1 43.4 %collective-permute-start.16 = (bf16[2,2,96,384]{3,2,1,0:T(8,128)(2,1)}, bf16[2,2,96,384]{3,2,1,0:T(8,128)(2,1)S(1)}, u32[]{:S(2)}, u32[]{:S(2)}) collective-permute-start(bf16[2,2,96,384]{3,2,1,0:T(8,128)(2,1)} %get-tuple-element.112), channel_id=1, source_target_pairs={{0,4},{4,0},{8,12},{12,8},{16,20},{20,16},{24,28},{28,24},{1,5},{5... | collective-permute-start | bytes 884744 | tf_op jit(solution)/shard_map/ppermute | solution.py:1027
  185.5 24.5 %collective-permute-start.19 = (bf16[2,2,96,384]{3,2,1,0:T(8,128)(2,1)}, bf16[2,2,96,384]{3,2,1,0:T(8,128)(2,1)S(1)}, u32[]{:S(2)}, u32[]{:S(2)}) collective-permute-start(bf16[2,2,96,384]{3,2,1,0:T(8,128)(2,1)} %get-tuple-element.114), channel_id=1, source_target_pairs={{0,4},{4,0},{8,12},{12,8},{16,20},{20,16},{24,28},{28,24},{1,5},{5... | collective-permute-start | bytes 884744 | tf_op jit(solution)/shard_map/ppermute | solution.py:1027
  210.1 8.6 %collective-permute-start.20 = (bf16[1,1,1,2,96,384]{5,4,3,2,1,0:T(8,128)(2,1)S(1)}, bf16[1,1,1,2,96,384]{5,4,3,2,1,0:T(8,128)(2,1)S(1)}, u32[]{:S(2)}, u32[]{:S(2)}) collective-permute-start(bf16[1,1,1,2,96,384]{5,4,3,2,1,0:T(8,128)(2,1)S(1)} %fusion.5), channel_id=1, source_target_pairs={{0,8},{4,12},{8,0},{12,4},{16,24},{20,28},{24,16},{28,20},{1,9},{5... | collective-permute-start | bytes 442376 | tf_op jit(solution)/shard_map/ppermute | solution.py:731
  220.6 8.9 %collective-permute-start.9 = (bf16[1024,384]{1,0:T(8,128)(2,1)S(1)}, bf16[1024,384]{1,0:T(8,128)(2,1)S(1)}, u32[]{:S(2)}, u32[]{:S(2)}) collective-permute-start(bf16[1024,384]{1,0:T(8,128)(2,1)S(1)} %copy-done.32), channel_id=1, source_target_pairs={{0,1},{1,0},{2,3},{3,2},{4,5},{5,4},{6,7},{7,6},{8,9},{9,8},{10,11... | collective-permute-start | bytes 2359304 | tf_op jit(solution)/shard_map/ppermute | solution.py:813
  229.5 23.2 %collective-permute-start.24 = (bf16[1,1,1,1,96,384]{5,4,3,2,1,0:T(8,128)(2,1)}, bf16[1,1,1,1,96,384]{5,4,3,2,1,0:T(8,128)(2,1)S(1)}, u32[]{:S(2)}, u32[]{:S(2)}) collective-permute-start(bf16[1,1,1,1,96,384]{5,4,3,2,1,0:T(8,128)(2,1)} %fusion.9), channel_id=1, source_target_pairs={{0,16},{4,20},{8,24},{12,28},{16,0},{20,4},{24,8},{28,12},{1,17},{... | collective-permute-start | bytes 221192 | tf_op jit(solution)/shard_map/ppermute | solution.py:731
  240.2 50.7 %collective-permute-start.28 = (bf16[1,2,2,2,720,128]{5,4,3,2,1,0:T(8,128)(2,1)S(1)}, bf16[1,2,2,2,720,128]{5,4,3,2,1,0:T(8,128)(2,1)}, u32[]{:S(2)}, u32[]{:S(2)}) collective-permute-start(bf16[1,2,2,2,720,128]{5,4,3,2,1,0:T(8,128)(2,1)S(1)} %add_convert_fusion), channel_id=1, source_target_pairs={{0,2},{1,3},{2,0},{3,1},{4,6},{5,7},{6,4},{7,5},{8,10},{9,11},{10,... | collective-permute-start | bytes 4423688 | tf_op jit(solution)/shard_map/ppermute | solution.py:731
  243.4 44.6 %collective-permute-start.33 = (bf16[2,1,2,2,576,128]{5,4,3,2,1,0:T(8,128)(2,1)}, bf16[2,1,2,2,576,128]{5,4,3,2,1,0:T(8,128)(2,1)}, u32[]{:S(2)}, u32[]{:S(2)}) collective-permute-start(bf16[2,1,2,2,576,128]{5,4,3,2,1,0:T(8,128)(2,1)} %add_convert_fusion.1), channel_id=1, source_target_pairs={{0,4},{4,0},{8,12},{12,8},{16,20},{20,16},{24,28},{28,24},{1,5},{5... | collective-permute-start | bytes 3538952 | tf_op jit(solution)/shard_map/ppermute | solution.py:731
  253.9 22.7 %collective-permute-start.12 = (f32[18,768]{1,0:T(8,128)S(1)}, f32[18,768]{1,0:T(8,128)S(1)}, u32[]{:S(2)}, u32[]{:S(2)}) collective-permute-start(f32[18,768]{1,0:T(8,128)S(1)} %add.444), channel_id=1, source_target_pairs={{0,2},{1,3},{2,0},{3,1},{4,6},{5,7},{6,4},{7,5},{8,10},{9,11},{10,... | collective-permute-start | bytes 165896 | tf_op jit(solution)/shard_map/ppermute | solution.py:740
  282.7 10.9 %collective-permute-start.25 = (bf16[3,96,192]{1,2,0:T(8,128)(2,1)S(1)}, bf16[3,96,192]{1,2,0:T(8,128)(2,1)S(1)}, u32[]{:S(2)}, u32[]{:S(2)}) collective-permute-start(bf16[3,96,192]{1,2,0:T(8,128)(2,1)S(1)} %fusion.8), channel_id=1, source_target_pairs={{2,0},{0,1},{3,2},{1,3},{6,4},{4,5},{7,6},{5,7},{10,8},{8,9},{11,1... | collective-permute-start | bytes 331784 | tf_op jit(solution)/shard_map/ppermute | solution.py:1035
  282.8 10.9 %collective-permute-start.26 = (bf16[3,96,192]{1,2,0:T(8,128)(2,1)S(1)}, bf16[3,96,192]{1,2,0:T(8,128)(2,1)S(1)}, u32[]{:S(2)}, u32[]{:S(2)}) collective-permute-start(bf16[3,96,192]{1,2,0:T(8,128)(2,1)S(1)} %fusion.7), channel_id=1, source_target_pairs={{2,1},{1,2},{6,5},{5,6},{10,9},{9,10},{14,13},{13,14},{18,17},{17,... | collective-permute-start | bytes 331784 | tf_op jit(solution)/shard_map/ppermute | solution.py:1038
  285.4 10.7 %collective-permute-start.15 = (f32[18,768]{1,0:T(8,128)S(1)}, f32[18,768]{1,0:T(8,128)S(1)}, u32[]{:S(2)}, u32[]{:S(2)}) collective-permute-start(f32[18,768]{1,0:T(8,128)S(1)} %add.447), channel_id=1, source_target_pairs={{0,16},{4,20},{8,24},{12,28},{16,0},{20,4},{24,8},{28,12},{1,17},{... | collective-permute-start | bytes 165896 | tf_op jit(solution)/shard_map/ppermute | solution.py:740
  290.5 16.5 %collective-permute-start.34 = (bf16[1,1,2,2,576,128]{5,4,3,2,1,0:T(8,128)(2,1)}, bf16[1,1,2,2,576,128]{5,4,3,2,1,0:T(8,128)(2,1)S(1)}, u32[]{:S(2)}, u32[]{:S(2)}) collective-permute-start(bf16[1,1,2,2,576,128]{5,4,3,2,1,0:T(8,128)(2,1)} %add_convert_fusion.3), channel_id=1, source_target_pairs={{0,2},{1,3},{2,0},{3,1},{4,6},{5,7},{6,4},{7,5},{8,10},{9,11},{10,... | collective-permute-start | bytes 1769480 | tf_op jit(solution)/shard_map/ppermute | solution.py:731
  292.8 17.5 %collective-permute-start.29 = (bf16[1,1,2,2,720,128]{5,4,3,2,1,0:T(8,128)(2,1)S(1)}, bf16[1,1,2,2,720,128]{5,4,3,2,1,0:T(8,128)(2,1)S(1)}, u32[]{:S(2)}, u32[]{:S(2)}) collective-permute-start(bf16[1,1,2,2,720,128]{5,4,3,2,1,0:T(8,128)(2,1)S(1)} %add_convert_fusion.2), channel_id=1, source_target_pairs={{0,4},{4,0},{8,12},{12,8},{16,20},{20,16},{24,28},{28,24},{1,5},{5... | collective-permute-start | bytes 2211848 | tf_op jit(solution)/shard_map/ppermute | solution.py:731
  294.6 27.7 %collective-permute-start.10 = (bf16[512,768]{1,0:T(8,128)(2,1)}, bf16[512,768]{1,0:T(8,128)(2,1)S(1)}, u32[]{:S(2)}, u32[]{:S(2)}) collective-permute-start(bf16[512,768]{1,0:T(8,128)(2,1)} %get-tuple-element.102), channel_id=1, source_target_pairs={{0,2},{1,3},{2,0},{3,1},{4,6},{5,7},{6,4},{7,5},{8,10},{9,11},{10,... | collective-permute-start | bytes 2359304 | tf_op jit(solution)/shard_map/ppermute | solution.py:816
  308.3 14.2 %collective-permute-start.35 = (bf16[1,1,1,2,576,128]{5,4,3,2,1,0:T(8,128)(2,1)S(1)}, bf16[1,1,1,2,576,128]{5,4,3,2,1,0:T(8,128)(2,1)S(1)}, u32[]{:S(2)}, u32[]{:S(2)}) collective-permute-start(bf16[1,1,1,2,576,128]{5,4,3,2,1,0:T(8,128)(2,1)S(1)} %add_convert_fusion.5), channel_id=1, source_target_pairs={{0,8},{4,12},{8,0},{12,4},{16,24},{20,28},{24,16},{28,20},{1,9},{5... | collective-permute-start | bytes 884744 | tf_op jit(solution)/shard_map/ppermute | solution.py:731
  311.7 15.1 %collective-permute-start.30 = (bf16[1,1,1,2,720,128]{5,4,3,2,1,0:T(8,128)(2,1)S(1)}, bf16[1,1,1,2,720,128]{5,4,3,2,1,0:T(8,128)(2,1)S(1)}, u32[]{:S(2)}, u32[]{:S(2)}) collective-permute-start(bf16[1,1,1,2,720,128]{5,4,3,2,1,0:T(8,128)(2,1)S(1)} %add_convert_fusion.4), channel_id=1, source_target_pairs={{0,8},{4,12},{8,0},{12,4},{16,24},{20,28},{24,16},{28,20},{1,9},{5... | collective-permute-start | bytes 1105928 | tf_op jit(solution)/shard_map/ppermute | solution.py:731
  323.7 14.6 %collective-permute-start.36 = (bf16[1,1,1,1,576,128]{5,4,3,2,1,0:T(8,128)(2,1)S(1)}, bf16[1,1,1,1,576,128]{5,4,3,2,1,0:T(8,128)(2,1)S(1)}, u32[]{:S(2)}, u32[]{:S(2)}) collective-permute-start(bf16[1,1,1,1,576,128]{5,4,3,2,1,0:T(8,128)(2,1)S(1)} %add_convert_fusion.7), channel_id=1, source_target_pairs={{0,16},{4,20},{8,24},{12,28},{16,0},{20,4},{24,8},{28,12},{1,17},{... | collective-permute-start | bytes 442376 | tf_op jit(solution)/shard_map/ppermute | solution.py:731
  328.0 12.8 %collective-permute-start.31 = (bf16[1,1,1,1,720,128]{5,4,3,2,1,0:T(8,128)(2,1)S(1)}, bf16[1,1,1,1,720,128]{5,4,3,2,1,0:T(8,128)(2,1)S(1)}, u32[]{:S(2)}, u32[]{:S(2)}) collective-permute-start(bf16[1,1,1,1,720,128]{5,4,3,2,1,0:T(8,128)(2,1)S(1)} %add_convert_fusion.6), channel_id=1, source_target_pairs={{0,16},{4,20},{8,24},{12,28},{16,0},{20,4},{24,8},{28,12},{1,17},{... | collective-permute-start | bytes 552968 | tf_op jit(solution)/shard_map/ppermute | solution.py:731
  (49 other events, 500.4 us)
